TPU v7x, 768 devices: a whole 4x8x12 slice. The times are simulated.
768 devices in a mesh: replica: 32 (over y, x), owner: 6 (over z_lo, core), tensor: 4 (over z_hi).
Axes of the slice: x: 4, y: 8, z: 12 (z_hi: 4, z_lo: 3; z = z_hi * 3 + z_lo), core: 2. Of those that a mesh axis runs over, the one named last changes fastest.
Arguments:
- grad_partial: bfloat16 [192, 24, 512, 512], P(('replica', 'owner'), 'tensor'), may hold values from -1 to 1
- owner_table: int32 [4, 6], P('tensor'), may hold values from 0 to 5, each once within a row
- left_factor: float32 [6, 4, 512, 512], P('owner', 'tensor'), may hold values from -1 to 4, as said below
- right_factor: float32 [6, 4, 512, 512], P('owner', 'tensor'), may hold values from -1 to 4, as said below
- left_precond: bfloat16 [6, 4, 512, 512], P('owner', 'tensor'), may hold values from -2 to 3, as said below
- right_precond: bfloat16 [6, 4, 512, 512], P('owner', 'tensor'), may hold values from -2 to 3, as said below
Outputs:
- direction: bfloat16 [24, 512, 512], P('tensor')
- new_left: float32 [6, 4, 512, 512], P('owner', 'tensor')
- new_right: float32 [6, 4, 512, 512], P('owner', 'tensor')
Inputs may be any that keep to these rules, and one draw needn't show every extreme that they name: `owner_table`: each row of the table is a permutation: every owner holds exactly one block of each tensor shard. `left_factor`: Symmetric. `right_factor`: Symmetric. `left_precond`: Symmetric. `right_precond`: Symmetric.
All inputs are finite; a program needn't handle non-finite values.
Results may differ from a plain program's by a relative error of at most 0.015.
Values may be sent and summed in bfloat16 or wider, within the bound.
No kernel may reach another device: no remote copies, remote signals or barrier semaphores. Data moves between devices by JAX's collectives and lax.ppermute only.
A program may use at most 32 MiB of HBM per device.

v0:
```python
import functools

import jax
import jax.numpy as jnp
from jax import lax
from jax.experimental import pallas as pl
from jax.experimental.pallas import tpu as pltpu
from jax.sharding import Mesh, PartitionSpec as P


decay = 0.9
epsilon = 1e-06

NY, NX, NZ, NC, NT = 8, 4, 3, 2, 4
B = 512
ROWS = B // (NX * NY)
SWAP = [(0, 1), (1, 0)]
VMEM = pltpu.MemorySpace.VMEM
HBM = pltpu.MemorySpace.HBM
SMEM = pltpu.MemorySpace.SMEM


def block_of(table_ref, owner):
    found = jnp.int32(0)
    for k in range(NZ * NC):
        found = jnp.where(table_ref[0, k] == owner, jnp.int32(k), found)
    return found


def call(kernel, out, scalars, arrays, scratch=(), cost=0, space=VMEM):
    held = [pltpu.with_memory_space_constraint(a, space) for a in arrays]
    return pl.pallas_call(
        kernel,
        out_shape=pltpu.VMEM(out, jnp.bfloat16),
        in_specs=[pl.BlockSpec(memory_space=SMEM)] * len(scalars)
        + [pl.BlockSpec(memory_space=space)] * len(arrays),
        out_specs=pl.BlockSpec(memory_space=VMEM),
        scratch_shapes=list(scratch),
        compiler_params=pltpu.CompilerParams(vmem_limit_bytes=2**22),
        cost_estimate=pl.CostEstimate(flops=0, bytes_accessed=cost, transcendentals=0),
    )(*scalars, *held)


def give_kernel(table_ref, place_ref, grad_ref, out_ref, sem):
    copies = [
        pltpu.make_async_copy(
            grad_ref.at[block_of(table_ref, 2 * z + 1 - place_ref[0])], out_ref.at[z], sem.at[z]
        )
        for z in range(NZ)
    ]
    for copy in copies:
        copy.start()
    for copy in copies:
        copy.wait()


def pair_kernel(table_ref, place_ref, grad_ref, got_ref, out_ref):
    for z in range(NZ):
        mine = block_of(table_ref, 2 * z + place_ref[0])
        for piece in range(NX * NY):
            rows = pl.ds(piece * ROWS, ROWS)
            total = grad_ref[mine, rows].astype(jnp.float32) + got_ref[z, rows].astype(jnp.float32)
            out_ref[piece % NX, piece // NX, z] = total.astype(out_ref.dtype)


def sum_kernel(terms_ref, out_ref):
    count, pieces = terms_ref.shape[0], terms_ref.shape[1]

    def step(i, carry):
        total = terms_ref[0, i].astype(jnp.float32)
        for t in range(1, count):
            total = total + terms_ref[t, i].astype(jnp.float32)
        out_ref[i] = total.astype(out_ref.dtype)
        return carry

    lax.fori_loop(0, pieces, step, 0, unroll=2)


def spread_kernel(terms_ref, out_ref):
    total = terms_ref[0].astype(jnp.float32)
    for t in range(1, terms_ref.shape[0]):
        total = total + terms_ref[t].astype(jnp.float32)
    strip = total.astype(out_ref.dtype)
    for i in range(out_ref.shape[0]):
        out_ref[i] = strip


def direction_kernel(left_ref, owned_ref, right_ref, out_ref, full_ref):
    step = 128
    square = jnp.zeros((8, 128), jnp.float32)
    for i in range(B // step):
        rows = pl.ds(i * step, step)
        half = jnp.dot(left_ref[rows], owned_ref[...], preferred_element_type=jnp.float32)
        full = jnp.dot(half.astype(jnp.bfloat16), right_ref[...], preferred_element_type=jnp.float32)
        full_ref[rows] = full
        square = square + jnp.sum((full * full).reshape(step // 8, 8, B // 128, 128), axis=(0, 2))
    scale = lax.rsqrt(jnp.sum(square) * (1.0 / (B * B)) + epsilon)
    for i in range(B // step):
        rows = pl.ds(i * step, step)
        out_ref[rows] = (full_ref[rows] * scale).astype(out_ref.dtype)


def place_kernel(hops, table_ref, place_ref, *refs):
    count = len(hops)
    blocks, out_ref, sem = refs[:count], refs[-2], refs[-1]
    copies = []
    for i, (d, s) in enumerate(hops):
        core = place_ref[0] if s == 0 else 1 - place_ref[0]
        z = lax.rem(place_ref[1] + NZ - d, jnp.int32(NZ))
        copies.append(
            pltpu.make_async_copy(blocks[i], out_ref.at[block_of(table_ref, 2 * z + core)], sem.at[i])
        )
    for copy in copies:
        copy.start()
    for copy in copies:
        copy.wait()


def place(table, here, hops, blocks, into=None):
    count = len(blocks)
    extra = [] if into is None else [into]
    held = [pltpu.with_memory_space_constraint(b, VMEM) for b in blocks]
    return pl.pallas_call(
        functools.partial(place_kernel, hops),
        out_shape=jax.ShapeDtypeStruct((NZ * NC, B, B), jnp.bfloat16),
        in_specs=[pl.BlockSpec(memory_space=SMEM)] * 2
        + [pl.BlockSpec(memory_space=VMEM)] * count
        + [pl.BlockSpec(memory_space=pl.ANY)] * len(extra),
        out_specs=pl.BlockSpec(memory_space=pl.ANY),
        scratch_shapes=[pltpu.SemaphoreType.DMA((count,))],
        input_output_aliases={2 + count: 0} if extra else {},
        compiler_params=pltpu.CompilerParams(vmem_limit_bytes=2**22),
        cost_estimate=pl.CostEstimate(flops=0, bytes_accessed=2 * count * B * B, transcendentals=0),
        name="place",
    )(table, here, *held, *extra)


def step(grad_partial, owner_table, left_factor, right_factor, left_precond, right_precond):
    core = lax.axis_index("core")
    here = jnp.stack([core, lax.axis_index("zl")]).astype(jnp.int32)

    give = call(
        give_kernel,
        (NZ, B, B),
        (owner_table, here),
        (grad_partial[0],),
        scratch=[pltpu.SemaphoreType.DMA((NZ,))],
        cost=2**21,
        space=HBM,
    )
    got = lax.ppermute(give, "core", SWAP)
    pieces = call(
        pair_kernel, (NX, NY, NZ, ROWS, B), (owner_table, here), (grad_partial[0], got), cost=2**22
    )
    over_x = lax.all_to_all(pieces.reshape(NX, NY * NZ, ROWS, B), "x", 0, 0)
    part = call(sum_kernel, (NY * NZ, ROWS, B), (), (over_x,), cost=2**21)
    over_yz = lax.all_to_all(part, ("y", "zl"), 0, 0)
    strips = call(spread_kernel, (NY * NX, ROWS, B), (), (over_yz,), cost=2**20)
    owned = lax.all_to_all(strips, ("y", "x"), 0, 0).reshape(B, B)

    scaled = call(
        direction_kernel,
        (B, B),
        (),
        (left_precond[0, 0], owned, right_precond[0, 0]),
        scratch=[pltpu.VMEM((B, B), jnp.float32)],
        cost=2**21,
    )
    near = lax.ppermute(scaled, "zl", [(z, (z + 1) % NZ) for z in range(NZ)])
    far = lax.ppermute(scaled, "zl", [(z, (z + 2) % NZ) for z in range(NZ)])
    scaled_other = lax.ppermute(scaled, "core", SWAP)
    near_other = lax.ppermute(near, "core", SWAP)
    early = [(0, 0), (1, 0), (0, 1), (1, 1)]
    direction = place(owner_table, here, early, [scaled, near, scaled_other, near_other])
    far_other = lax.ppermute(far, "core", SWAP)
    direction = place(owner_table, here, [(2, 0), (2, 1)], [far, far_other], direction)

    outer_rows = lax.dot_general(
        owned, owned, (((1,), (1,)), ((), ())), preferred_element_type=jnp.float32
    )
    new_left = (decay * left_factor[0, 0] + (1.0 - decay) * outer_rows)[None, None]
    outer_cols = lax.dot_general(
        owned, owned, (((0,), (0,)), ((), ())), preferred_element_type=jnp.float32
    )
    new_right = (decay * right_factor[0, 0] + (1.0 - decay) * outer_cols)[None, None]
    return (direction, new_left, new_right)


def solution(mesh):
    fine = Mesh(mesh.devices.reshape(NY, NX, NZ, NC, NT), ("y", "x", "zl", "core", "tensor"))
    owner = ("zl", "core")
    placed = (
        P(("y", "x") + owner, "tensor", None, None),
        P("tensor", None),
        P(owner, "tensor", None, None),
        P(owner, "tensor", None, None),
        P(owner, "tensor", None, None),
        P(owner, "tensor", None, None),
    )
    return jax.shard_map(
        step,
        mesh=fine,
        in_specs=placed,
        out_specs=(
            P("tensor", None, None),
            P(owner, "tensor", None, None),
            P(owner, "tensor", None, None),
        ),
        check_vma=False,
    )
```

profile of v0, /device:TPU:1, one launch (start us, length us, event | category | flops | bytes accessed | tf_op | source)
XLA Modules:
  0.0 116.5 jit_solution(15258389429838257364)
XLA Ops:
  0.6 0.1 pad_add_fusion.place_ref
  0.7 0.7 copy-done.3
  1.4 2.2 %shard_map.85 = bf16[3,512,512]{2,1,0:T(8,128)(2,1)S(1)} custom-call(s32[1,6]{1,0:T(1,128)S(1)} %copy-done.3, s32[2]{0:T(128)S(1)} %pad_add_fusion.place_ref, bf16[6,512,512]{2,1,0:T(8,128)(2,1)} %bitcast.27), custom_call_target="tpu_custom_call" | custom-call | bytes 2097152 | tf_op jit(solution)/shard_map/pallas_call | solution.py:32
  3.6 12.4 %collective-permute-start = (bf16[3,512,512]{2,1,0:T(8,128)(2,1)S(1)}, bf16[3,512,512]{2,1,0:T(8,128)(2,1)S(1)}, u32[]{:S(2)}, u32[]{:S(2)}) collective-permute-start(bf16[3,512,512]{2,1,0:T(8,128)(2,1)S(1)} %shard_map.85), channel_id=1, source_target_pairs={{0,4},{4,0},{1,5},{5,1},{2,6},{6,2},{3,7},{7,3},{8,12},{12,8},{9,1... | collective-permute-start | bytes 4718600 | tf_op jit(solution)/shard_map/ppermute | solution.py:151
  16.0 3.0 %collective-permute-done.got_ref = bf16[3,512,512]{2,1,0:T(8,128)(2,1)S(1)} collective-permute-done((bf16[3,512,512]{2,1,0:T(8,128)(2,1)S(1)}, bf16[3,512,512]{2,1,0:T(8,128)(2,1)S(1)}, u32[]{:S(2)}, u32[]{:S(2)}) %collective-permute-start) | collective-permute-done | bytes 1572896 | tf_op jit(solution)/shard_map/ppermute | solution.py:151
  19.0 0.9 shard_map.86
  19.9 22.9 %all_to_all.15.terms_ref = bf16[4,24,16,512]{3,2,1,0:T(8,128)(2,1)S(1)} all-to-all(bf16[4,24,16,512]{3,2,1,0:T(8,128)(2,1)S(1)} %bitcast.31), channel_id=1, replica_groups=mesh['y'=8,'x'=4,'zl'=3,'core'=2,'tensor'=4] {'x'}, dimensions={0} | all-to-all | bytes 3145728 | tf_op jit(solution)/shard_map/all_to_all | solution.py:155
  42.8 0.2 shard_map.87
  43.0 0.0 copy-start.1
  43.1 15.0 %all_to_all.16.terms_ref = bf16[24,16,512]{2,1,0:T(8,128)(2,1)S(1)} all-to-all(bf16[24,16,512]{2,1,0:T(8,128)(2,1)S(1)} %shard_map.87), channel_id=1, replica_groups=mesh['y'=8,'x'=4,'zl'=3,'core'=2,'tensor'=4] {'y','zl'}, dimensions={0} | all-to-all | bytes 786432 | tf_op jit(solution)/shard_map/all_to_all | solution.py:157
  58.1 0.1 shard_map.88
  58.2 20.3 %all_to_all.17 = bf16[32,16,512]{2,1,0:T(8,128)(2,1)S(1)} all-to-all(bf16[32,16,512]{2,1,0:T(8,128)(2,1)S(1)} %shard_map.88), channel_id=1, replica_groups=mesh['y'=8,'x'=4,'zl'=3,'core'=2,'tensor'=4] {'y','x'}, dimensions={0} | all-to-all | bytes 1048576 | tf_op jit(solution)/shard_map/all_to_all | solution.py:159
  78.4 1.4 %shard_map.89.refs_0_ = bf16[512,512]{1,0:T(8,128)(2,1)S(1)} custom-call(bf16[512,512]{1,0:T(8,128)(2,1)S(1)} %bitcast.32, bf16[512,512]{1,0:T(8,128)(2,1)S(1)} %bitcast.29, bf16[512,512]{1,0:T(8,128)(2,1)S(1)} %bitcast.33), custom_call_target="tpu_custom_call" | custom-call | bytes 2097152 | tf_op jit(solution)/shard_map/pallas_call | solution.py:32
  79.9 3.3 %collective-permute-start.3 = (bf16[512,512]{1,0:T(8,128)(2,1)S(1)}, bf16[512,512]{1,0:T(8,128)(2,1)S(1)}, u32[]{:S(2)}, u32[]{:S(2)}) collective-permute-start(bf16[512,512]{1,0:T(8,128)(2,1)S(1)} %shard_map.89.refs_0_), channel_id=1, source_target_pairs={{0,8},{8,16},{16,0},{1,9},{9,17},{17,1},{2,10},{10,18},{18,2},{3,1... | collective-permute-start | bytes 1572872 | tf_op jit(solution)/shard_map/ppermute | solution.py:169
  83.2 4.3 %collective-permute-start.1 = (bf16[512,512]{1,0:T(8,128)(2,1)S(1)}, bf16[512,512]{1,0:T(8,128)(2,1)S(1)}, u32[]{:S(2)}, u32[]{:S(2)}) collective-permute-start(bf16[512,512]{1,0:T(8,128)(2,1)S(1)} %shard_map.89.refs_0_), channel_id=1, source_target_pairs={{0,16},{8,0},{16,8},{1,17},{9,1},{17,9},{2,18},{10,2},{18,10},{3,1... | collective-permute-start | bytes 1572872 | tf_op jit(solution)/shard_map/ppermute | solution.py:170
  87.5 4.5 %collective-permute-start.4 = (bf16[512,512]{1,0:T(8,128)(2,1)S(1)}, bf16[512,512]{1,0:T(8,128)(2,1)S(1)}, u32[]{:S(2)}, u32[]{:S(2)}) collective-permute-start(bf16[512,512]{1,0:T(8,128)(2,1)S(1)} %shard_map.89.refs_0_), channel_id=1, source_target_pairs={{0,4},{4,0},{1,5},{5,1},{2,6},{6,2},{3,7},{7,3},{8,12},{12,8},{9,1... | collective-permute-start | bytes 1572872 | tf_op jit(solution)/shard_map/ppermute | solution.py:171
  92.1 1.5 %fusion.2 = f32[1,1,512,512]{3,2,1,0:T(8,128)} fusion(bf16[512,512]{1,0:T(8,128)(2,1)S(1)} %bitcast.30, f32[1,1,512,512]{3,2,1,0:T(8,128)S(1)} %copy-done.5), kind=kOutput, calls=%fused_computation.4 | convolution fusion | flops 269221888 | bytes 2621440 | tf_op jit(solution)/shard_map/dot_general | solution.py:178
  93.5 2.1 %collective-permute-done.3.refs_1_ = bf16[512,512]{1,0:T(8,128)(2,1)S(1)} collective-permute-done((bf16[512,512]{1,0:T(8,128)(2,1)S(1)}, bf16[512,512]{1,0:T(8,128)(2,1)S(1)}, u32[]{:S(2)}, u32[]{:S(2)}) %collective-permute-start.3) | collective-permute-done | bytes 524320 | tf_op jit(solution)/shard_map/ppermute | solution.py:169
  95.6 7.3 %collective-permute-start.5 = (bf16[512,512]{1,0:T(8,128)(2,1)S(1)}, bf16[512,512]{1,0:T(8,128)(2,1)S(1)}, u32[]{:S(2)}, u32[]{:S(2)}) collective-permute-start(bf16[512,512]{1,0:T(8,128)(2,1)S(1)} %collective-permute-done.3.refs_1_), channel_id=1, source_target_pairs={{0,4},{4,0},{1,5},{5,1},{2,6},{6,2},{3,7},{7,3},{8,12},{12,8},{9,1... | collective-permute-start | bytes 1572872 | tf_op jit(solution)/shard_map/ppermute | solution.py:172
  102.9 6.3 %collective-permute-done.1.refs_0_ = bf16[512,512]{1,0:T(8,128)(2,1)S(1)} collective-permute-done((bf16[512,512]{1,0:T(8,128)(2,1)S(1)}, bf16[512,512]{1,0:T(8,128)(2,1)S(1)}, u32[]{:S(2)}, u32[]{:S(2)}) %collective-permute-start.1) | collective-permute-done | bytes 524320 | tf_op jit(solution)/shard_map/ppermute | solution.py:170
  109.2 2.4 %collective-permute-start.2 = (bf16[512,512]{1,0:T(8,128)(2,1)S(1)}, bf16[512,512]{1,0:T(8,128)(2,1)S(1)}, u32[]{:S(2)}, u32[]{:S(2)}) collective-permute-start(bf16[512,512]{1,0:T(8,128)(2,1)S(1)} %collective-permute-done.1.refs_0_), channel_id=1, source_target_pairs={{0,4},{4,0},{1,5},{5,1},{2,6},{6,2},{3,7},{7,3},{8,12},{12,8},{9,1... | collective-permute-start | bytes 1572872 | tf_op jit(solution)/shard_map/ppermute | solution.py:175
  111.6 1.5 %fusion.4 = f32[1,1,512,512]{3,2,1,0:T(8,128)} fusion(bf16[32,16,512]{2,1,0:T(8,128)(2,1)S(1)} %all_to_all.17, f32[1,1,512,512]{3,2,1,0:T(8,128)S(1)} %copy-done.6), kind=kOutput, calls=%fused_computation.6 | convolution fusion | flops 269221888 | bytes 2621440 | tf_op jit(solution)/shard_map/dot_general | solution.py:182
  113.1 1.9 %place.2.refs_2_ = bf16[6,512,512]{2,1,0:T(8,128)(2,1)} custom-call(s32[1,6]{1,0:T(1,128)S(1)} %copy-done.4, s32[2]{0:T(128)S(1)} %pad_add_fusion.place_ref, bf16[512,512]{1,0:T(8,128)(2,1)S(1)} %shard_map.89.refs_0_, bf16[512,512]{1,0:T(8,128)(2,1)S(1)} %collective-permute-done.3.refs_1_, bf16[512,512]{1,0:T(8,128)(2,1)S(1)} %collective-permute-done.4.refs_2_, ...), custom_call_target="tpu_custom_call" | custom-call | bytes 2097152 | tf_op jit(solution)/shard_map/place/pallas_call | solution.py:123
  115.0 1.5 %place.3 = bf16[6,512,512]{2,1,0:T(8,128)(2,1)} custom-call(s32[1,6]{1,0:T(1,128)S(1)} %copy-done.4, s32[2]{0:T(128)S(1)} %pad_add_fusion.place_ref, bf16[512,512]{1,0:T(8,128)(2,1)S(1)} %collective-permute-done.1.refs_0_, bf16[512,512]{1,0:T(8,128)(2,1)S(1)} %collective-permute-done.2.refs_1_, ...), custom_call_target="tpu_custom_call", output_to_operand_aliasing={{}: (4, {})} | custom-call | bytes 1048576 | tf_op jit(solution)/shard_map/place/pallas_call | solution.py:123
  (15 shorter events, 0.0 us)
Async XLA Ops:
  0.7 0.7 copy-start.3
  1.4 17.6 %copy-start = (bf16[1,6,512,512]{3,2,1,0:T(8,128)(2,1)S(1)}, bf16[1,6,512,512]{3,2,1,0:T(8,128)(2,1)}, u32[]{:S(2)}) copy-start(bf16[1,6,512,512]{3,2,1,0:T(8,128)(2,1)} %param.6) | copy-start | bytes 9437188
  3.6 15.4 %collective-permute-start = (bf16[3,512,512]{2,1,0:T(8,128)(2,1)S(1)}, bf16[3,512,512]{2,1,0:T(8,128)(2,1)S(1)}, u32[]{:S(2)}, u32[]{:S(2)}) collective-permute-start(bf16[3,512,512]{2,1,0:T(8,128)(2,1)S(1)} %shard_map.85), channel_id=1, source_target_pairs={{0,4},{4,0},{1,5},{5,1},{2,6},{6,2},{3,7},{7,3},{8,12},{12,8},{9,1... | collective-permute-start | bytes 4718600 | tf_op jit(solution)/shard_map/ppermute | solution.py:151
  43.0 35.4 %copy-start.1 = (bf16[1,1,512,512]{3,2,1,0:T(8,128)(2,1)S(1)}, bf16[1,1,512,512]{3,2,1,0:T(8,128)(2,1)}, u32[]{:S(2)}) copy-start(bf16[1,1,512,512]{3,2,1,0:T(8,128)(2,1)} %param.10) | copy-start | bytes 1572868
  43.1 35.4 %copy-start.2 = (bf16[1,1,512,512]{3,2,1,0:T(8,128)(2,1)S(1)}, bf16[1,1,512,512]{3,2,1,0:T(8,128)(2,1)}, u32[]{:S(2)}) copy-start(bf16[1,1,512,512]{3,2,1,0:T(8,128)(2,1)} %param.11) | copy-start | bytes 1572868
  58.2 33.9 %copy-start.5 = (f32[1,1,512,512]{3,2,1,0:T(8,128)S(1)}, f32[1,1,512,512]{3,2,1,0:T(8,128)}, u32[]{:S(2)}) copy-start(f32[1,1,512,512]{3,2,1,0:T(8,128)} %param.8) | copy-start | bytes 3145732
  79.9 31.7 %copy-start.6 = (f32[1,1,512,512]{3,2,1,0:T(8,128)S(1)}, f32[1,1,512,512]{3,2,1,0:T(8,128)}, u32[]{:S(2)}) copy-start(f32[1,1,512,512]{3,2,1,0:T(8,128)} %param.9) | copy-start | bytes 3145732
  79.9 15.7 %collective-permute-start.3 = (bf16[512,512]{1,0:T(8,128)(2,1)S(1)}, bf16[512,512]{1,0:T(8,128)(2,1)S(1)}, u32[]{:S(2)}, u32[]{:S(2)}) collective-permute-start(bf16[512,512]{1,0:T(8,128)(2,1)S(1)} %shard_map.89.refs_0_), channel_id=1, source_target_pairs={{0,8},{8,16},{16,0},{1,9},{9,17},{17,1},{2,10},{10,18},{18,2},{3,1... | collective-permute-start | bytes 1572872 | tf_op jit(solution)/shard_map/ppermute | solution.py:169
  83.2 26.0 %collective-permute-start.1 = (bf16[512,512]{1,0:T(8,128)(2,1)S(1)}, bf16[512,512]{1,0:T(8,128)(2,1)S(1)}, u32[]{:S(2)}, u32[]{:S(2)}) collective-permute-start(bf16[512,512]{1,0:T(8,128)(2,1)S(1)} %shard_map.89.refs_0_), channel_id=1, source_target_pairs={{0,16},{8,0},{16,8},{1,17},{9,1},{17,9},{2,18},{10,2},{18,10},{3,1... | collective-permute-start | bytes 1572872 | tf_op jit(solution)/shard_map/ppermute | solution.py:170
  87.5 25.5 %collective-permute-start.4 = (bf16[512,512]{1,0:T(8,128)(2,1)S(1)}, bf16[512,512]{1,0:T(8,128)(2,1)S(1)}, u32[]{:S(2)}, u32[]{:S(2)}) collective-permute-start(bf16[512,512]{1,0:T(8,128)(2,1)S(1)} %shard_map.89.refs_0_), channel_id=1, source_target_pairs={{0,4},{4,0},{1,5},{5,1},{2,6},{6,2},{3,7},{7,3},{8,12},{12,8},{9,1... | collective-permute-start | bytes 1572872 | tf_op jit(solution)/shard_map/ppermute | solution.py:171
  93.5 19.6 %copy-start.4 = (s32[1,6]{1,0:T(1,128)S(1)}, s32[1,6]{1,0:T(1,128)}, u32[]{:S(2)}) copy-start(s32[1,6]{1,0:T(1,128)} %table_ref.7) | copy-start | bytes 76
  95.6 17.5 %collective-permute-start.5 = (bf16[512,512]{1,0:T(8,128)(2,1)S(1)}, bf16[512,512]{1,0:T(8,128)(2,1)S(1)}, u32[]{:S(2)}, u32[]{:S(2)}) collective-permute-start(bf16[512,512]{1,0:T(8,128)(2,1)S(1)} %collective-permute-done.3.refs_1_), channel_id=1, source_target_pairs={{0,4},{4,0},{1,5},{5,1},{2,6},{6,2},{3,7},{7,3},{8,12},{12,8},{9,1... | collective-permute-start | bytes 1572872 | tf_op jit(solution)/shard_map/ppermute | solution.py:172
  109.2 5.8 %collective-permute-start.2 = (bf16[512,512]{1,0:T(8,128)(2,1)S(1)}, bf16[512,512]{1,0:T(8,128)(2,1)S(1)}, u32[]{:S(2)}, u32[]{:S(2)}) collective-permute-start(bf16[512,512]{1,0:T(8,128)(2,1)S(1)} %collective-permute-done.1.refs_0_), channel_id=1, source_target_pairs={{0,4},{4,0},{1,5},{5,1},{2,6},{6,2},{3,7},{7,3},{8,12},{12,8},{9,1... | collective-permute-start | bytes 1572872 | tf_op jit(solution)/shard_map/ppermute | solution.py:175
where the time goes:
time: 118 us; the launch traced here: 117 us
  blocking collectives  58.1 us (49%)
  starting transfers between devices  34.2 us (29%)
  waiting for transfers between devices  11.4 us (10%)
  Pallas kernels  8.34 us (7%)
  matrix products  2.91 us (2%)
    all_to_all x1, blocking collectives, step(): over_x = lax.all_to_all(pieces.reshape(NX, NY * NZ, ROWS, B), 'x', 0, 0)  22.9 us
    all_to_all x1, blocking collectives, step(): owned = lax.all_to_all(strips, ('y', 'x'), 0, 0).reshape(B, B)  20.3 us
    all_to_all x1, blocking collectives, step(): over_yz = lax.all_to_all(part, ('y', 'zl'), 0, 0)  15 us
    ppermute x1, starting transfers between devices, step(): got = lax.ppermute(give, 'core', SWAP)  12.4 us
    ppermute x1, starting transfers between devices, step(): near_other = lax.ppermute(near, 'core', SWAP)  7.3 us
    ppermute x1, waiting for transfers between devices, step(): far = lax.ppermute(scaled, 'zl', [(z, (z + 2) % NZ) for z in range(NZ)])  6.29 us
    pallas_call x5, Pallas kernels, call(): pl.pallas_call(kernel, out_shape=pltpu.VMEM(out, jnp.bfloat16), in_specs=...  4.89 us
    ppermute x1, starting transfers between devices, step(): scaled_other = lax.ppermute(scaled, 'core', SWAP)  4.51 us
  transfers between devices with their start and end apart: 6, of which 3 were waited for; matrix products, arithmetic and copies ran while one was open for 2% of the time, Pallas kernels for 2%

commit v1 on v0

--- a/solution.py
+++ b/solution.py
@@ -14,10 +14,25 @@
 NY, NX, NZ, NC, NT = 8, 4, 3, 2, 4
 B = 512
 ROWS = B // (NX * NY)
+NEAR, AWAY = 4, 8
 SWAP = [(0, 1), (1, 0)]
+SLAB = ("y", "x", "zl", "core")
 VMEM = pltpu.MemorySpace.VMEM
 HBM = pltpu.MemorySpace.HBM
 SMEM = pltpu.MemorySpace.SMEM
+
+
+def device(core, height, quad, member):
+    y = (2 * (quad // 2) + member // 2 + core) % NY
+    x = (2 * (quad % 2) + member % 2 + core) % NX
+    return ((y * NX + x) * NZ + height) * NC + core
+
+
+QUADS = [[device(c, z, f, q) for q in range(NEAR)] for c in range(NC) for z in range(NZ) for f in range(AWAY)]
+AWAYS = [[device(c, z, f, q) for f in range(AWAY)] for c in range(NC) for z in range(NZ) for q in range(NEAR)]
+AWAY_Z = [
+    [device(c, z, f, q) for f in range(AWAY) for z in range(NZ)] for c in range(NC) for q in range(NEAR)
+]
 
 
 def block_of(table_ref, owner):
@@ -31,10 +46,14 @@
     held = [pltpu.with_memory_space_constraint(a, space) for a in arrays]
     return pl.pallas_call(
         kernel,
-        out_shape=pltpu.VMEM(out, jnp.bfloat16),
+        out_shape=tuple(pltpu.VMEM(o, jnp.bfloat16) for o in out)
+        if isinstance(out[0], tuple)
+        else pltpu.VMEM(out, jnp.bfloat16),
         in_specs=[pl.BlockSpec(memory_space=SMEM)] * len(scalars)
         + [pl.BlockSpec(memory_space=space)] * len(arrays),
-        out_specs=pl.BlockSpec(memory_space=VMEM),
+        out_specs=(pl.BlockSpec(memory_space=VMEM),) * len(out)
+        if isinstance(out[0], tuple)
+        else pl.BlockSpec(memory_space=VMEM),
         scratch_shapes=list(scratch),
         compiler_params=pltpu.CompilerParams(vmem_limit_bytes=2**22),
         cost_estimate=pl.CostEstimate(flops=0, bytes_accessed=cost, transcendentals=0),
@@ -60,7 +79,7 @@
         for piece in range(NX * NY):
             rows = pl.ds(piece * ROWS, ROWS)
             total = grad_ref[mine, rows].astype(jnp.float32) + got_ref[z, rows].astype(jnp.float32)
-            out_ref[piece % NX, piece // NX, z] = total.astype(out_ref.dtype)
+            out_ref[piece // AWAY, piece % AWAY, z] = total.astype(out_ref.dtype)
 
 
 def sum_kernel(terms_ref, out_ref):
@@ -85,59 +104,77 @@
         out_ref[i] = strip
 
 
-def direction_kernel(left_ref, owned_ref, right_ref, out_ref, full_ref):
-    step = 128
+def repeat_kernel(strip_ref, out_ref):
+    for i in range(out_ref.shape[0]):
+        out_ref[i] = strip_ref[...]
+
+
+def foreign_kernel(place_ref, strips_ref, out_ref):
+    for d in range(1, NZ):
+        strip = strips_ref[lax.rem(place_ref[1] + NZ - d, jnp.int32(NZ))]
+        for i in range(out_ref.shape[0]):
+            out_ref[i, d - 1] = strip
+
+
+def direction_kernel(place_ref, left_ref, owned_ref, right_ref, out_ref, strips_ref, full_ref):
+    step = B // NEAR
     square = jnp.zeros((8, 128), jnp.float32)
-    for i in range(B // step):
+    for i in range(NEAR):
         rows = pl.ds(i * step, step)
         half = jnp.dot(left_ref[rows], owned_ref[...], preferred_element_type=jnp.float32)
         full = jnp.dot(half.astype(jnp.bfloat16), right_ref[...], preferred_element_type=jnp.float32)
-        full_ref[rows] = full
+        full_ref[i] = full
         square = square + jnp.sum((full * full).reshape(step // 8, 8, B // 128, 128), axis=(0, 2))
     scale = lax.rsqrt(jnp.sum(square) * (1.0 / (B * B)) + epsilon)
-    for i in range(B // step):
-        rows = pl.ds(i * step, step)
-        out_ref[rows] = (full_ref[rows] * scale).astype(out_ref.dtype)
-
-
-def place_kernel(hops, table_ref, place_ref, *refs):
-    count = len(hops)
-    blocks, out_ref, sem = refs[:count], refs[-2], refs[-1]
+    for i in range(NEAR):
+        out_ref[i] = (full_ref[i] * scale).astype(out_ref.dtype)
+    strip = out_ref[place_ref[2]]
+    for z in range(NZ):
+        strips_ref[z] = strip
+
+
+def place_kernel(parts, table_ref, place_ref, *refs):
+    out_ref, sem = refs[-2], refs[-1]
     copies = []
-    for i, (d, s) in enumerate(hops):
+    for n, (i, d, s) in enumerate(parts):
         core = place_ref[0] if s == 0 else 1 - place_ref[0]
         z = lax.rem(place_ref[1] + NZ - d, jnp.int32(NZ))
-        copies.append(
-            pltpu.make_async_copy(blocks[i], out_ref.at[block_of(table_ref, 2 * z + core)], sem.at[i])
-        )
+        block = refs[i] if d == 0 else refs[i].at[:, d - 1]
+        to = out_ref.at[block_of(table_ref, 2 * z + core)]
+        copies.append(pltpu.make_async_copy(block, to, sem.at[n]))
     for copy in copies:
         copy.start()
     for copy in copies:
         copy.wait()
 
 
-def place(table, here, hops, blocks, into=None):
-    count = len(blocks)
+def place(table, here, parts, arrays, into=None):
+    count = len(arrays)
     extra = [] if into is None else [into]
-    held = [pltpu.with_memory_space_constraint(b, VMEM) for b in blocks]
+    held = [pltpu.with_memory_space_constraint(a, VMEM) for a in arrays]
     return pl.pallas_call(
-        functools.partial(place_kernel, hops),
-        out_shape=jax.ShapeDtypeStruct((NZ * NC, B, B), jnp.bfloat16),
+        functools.partial(place_kernel, parts),
+        out_shape=jax.ShapeDtypeStruct((NZ * NC, NEAR, B // NEAR, B), jnp.bfloat16),
         in_specs=[pl.BlockSpec(memory_space=SMEM)] * 2
         + [pl.BlockSpec(memory_space=VMEM)] * count
         + [pl.BlockSpec(memory_space=pl.ANY)] * len(extra),
         out_specs=pl.BlockSpec(memory_space=pl.ANY),
-        scratch_shapes=[pltpu.SemaphoreType.DMA((count,))],
+        scratch_shapes=[pltpu.SemaphoreType.DMA((len(parts),))],
         input_output_aliases={2 + count: 0} if extra else {},
         compiler_params=pltpu.CompilerParams(vmem_limit_bytes=2**22),
-        cost_estimate=pl.CostEstimate(flops=0, bytes_accessed=2 * count * B * B, transcendentals=0),
+        cost_estimate=pl.CostEstimate(flops=0, bytes_accessed=2 * len(parts) * B * B, transcendentals=0),
         name="place",
     )(table, here, *held, *extra)
 
 
+def exchange(pieces, groups):
+    return lax.all_to_all(pieces, SLAB, 0, 0, axis_index_groups=groups)
+
+
 def step(grad_partial, owner_table, left_factor, right_factor, left_precond, right_precond):
     core = lax.axis_index("core")
-    here = jnp.stack([core, lax.axis_index("zl")]).astype(jnp.int32)
+    quarter = 2 * ((lax.axis_index("y") + core) % 2) + (lax.axis_index("x") + core) % 2
+    here = jnp.stack([core, lax.axis_index("zl"), quarter]).astype(jnp.int32)
 
     give = call(
         give_kernel,
@@ -149,31 +186,30 @@
         space=HBM,
     )
     got = lax.ppermute(give, "core", SWAP)
-    pieces = call(
-        pair_kernel, (NX, NY, NZ, ROWS, B), (owner_table, here), (grad_partial[0], got), cost=2**22
-    )
-    over_x = lax.all_to_all(pieces.reshape(NX, NY * NZ, ROWS, B), "x", 0, 0)
-    part = call(sum_kernel, (NY * NZ, ROWS, B), (), (over_x,), cost=2**21)
-    over_yz = lax.all_to_all(part, ("y", "zl"), 0, 0)
-    strips = call(spread_kernel, (NY * NX, ROWS, B), (), (over_yz,), cost=2**20)
-    owned = lax.all_to_all(strips, ("y", "x"), 0, 0).reshape(B, B)
-
-    scaled = call(
+    pieces = call(pair_kernel, (NEAR, AWAY, NZ, ROWS, B), (owner_table, here), (grad_partial[0], got), cost=2**22)
+    in_quad = exchange(pieces.reshape(NEAR, AWAY * NZ, ROWS, B), QUADS)
+    part = call(sum_kernel, (AWAY * NZ, ROWS, B), (), (in_quad,), cost=2**21)
+    strips = call(spread_kernel, (AWAY, ROWS, B), (), (exchange(part, AWAY_Z),), cost=2**20)
+    strip = exchange(strips, AWAYS).reshape(B // NEAR, B)
+    strips = call(repeat_kernel, (NEAR, B // NEAR, B), (), (strip,), cost=2**20)
+    owned = exchange(strips, QUADS).reshape(B, B)
+
+    scaled, strips = call(
         direction_kernel,
-        (B, B),
-        (),
+        ((NEAR, B // NEAR, B), (NZ, B // NEAR, B)),
+        (here,),
         (left_precond[0, 0], owned, right_precond[0, 0]),
-        scratch=[pltpu.VMEM((B, B), jnp.float32)],
+        scratch=[pltpu.VMEM((NEAR, B // NEAR, B), jnp.float32)],
         cost=2**21,
     )
-    near = lax.ppermute(scaled, "zl", [(z, (z + 1) % NZ) for z in range(NZ)])
-    far = lax.ppermute(scaled, "zl", [(z, (z + 2) % NZ) for z in range(NZ)])
     scaled_other = lax.ppermute(scaled, "core", SWAP)
-    near_other = lax.ppermute(near, "core", SWAP)
-    early = [(0, 0), (1, 0), (0, 1), (1, 1)]
-    direction = place(owner_table, here, early, [scaled, near, scaled_other, near_other])
-    far_other = lax.ppermute(far, "core", SWAP)
-    direction = place(owner_table, here, [(2, 0), (2, 1)], [far, far_other], direction)
+    strips = lax.all_to_all(strips, "zl", 0, 0)
+    foreign = call(foreign_kernel, (NEAR, NZ - 1, B // NEAR, B), (here,), (strips,), cost=2**20)
+    foreign = exchange(foreign, QUADS)
+    direction = place(owner_table, here, [(0, 0, 0), (1, 0, 1)], [scaled, scaled_other])
+    foreign_other = lax.ppermute(foreign, "core", SWAP)
+    late = [(0, 1, 0), (0, 2, 0), (1, 1, 1), (1, 2, 1)]
+    direction = place(owner_table, here, late, [foreign, foreign_other], direction).reshape(NZ * NC, B, B)
 
     outer_rows = lax.dot_general(
         owned, owned, (((1,), (1,)), ((), ())), preferred_element_type=jnp.float32

time: 118 us -> 119 us (level)
  the two profiles are of different devices: /device:TPU:1 before, /device:TPU:193 now
where the time goes in v1:
time: 119 us; the launch traced here: 118 us
  blocking collectives  93.1 us (78%)
  Pallas kernels  9.54 us (8%)
  starting transfers between devices  8.2 us (7%)
  waiting for transfers between devices  3.02 us (3%)
  matrix products  2.89 us (2%)
    all_to_all x5, blocking collectives, exchange(): return lax.all_to_all(pieces, SLAB, 0, 0, axis_index_groups=groups)  81.5 us
    all_to_all x1, blocking collectives, step(): strips = lax.all_to_all(strips, 'zl', 0, 0)  11.7 us
    pallas_call x7, Pallas kernels, call(): pl.pallas_call(kernel, out_shape=tuple((pltpu.VMEM(o, jnp.bfloat16) for o...  6.09 us
    ppermute x1, starting transfers between devices, step(): foreign_other = lax.ppermute(foreign, 'core', SWAP)  3.56 us
    pallas_call x2, Pallas kernels, place(): pl.pallas_call(functools.partial(place_kernel, parts), out_shape=jax.Shap...  3.45 us
    ppermute x1, waiting for transfers between devices, step(): got = lax.ppermute(give, 'core', SWAP)  3.01 us
    ppermute x1, starting transfers between devices, step(): got = lax.ppermute(give, 'core', SWAP)  2.58 us
  transfers between devices with their start and end apart: 3, of which 1 were waited for; matrix products, arithmetic and copies ran while one was open for 2% of the time, Pallas kernels for 1%

profile of v1, /device:TPU:193, one launch (start us, length us, event | category | flops | bytes accessed | tf_op | source)
XLA Modules:
  0.0 118.3 jit_solution(8728567360502134315)
XLA Ops:
  0.7 0.1 pad_add_fusion.place_ref
  0.7 0.7 copy-done.3
  1.4 2.2 %shard_map.85 = bf16[3,512,512]{2,1,0:T(8,128)(2,1)S(1)} custom-call(s32[1,6]{1,0:T(1,128)S(1)} %copy-done.3, s32[3]{0:T(128)S(1)} %pad_add_fusion.place_ref, bf16[6,512,512]{2,1,0:T(8,128)(2,1)} %bitcast.32), custom_call_target="tpu_custom_call" | custom-call | bytes 2097152 | tf_op jit(solution)/shard_map/pallas_call | solution.py:47
  3.6 2.6 %collective-permute-start = (bf16[3,512,512]{2,1,0:T(8,128)(2,1)S(1)}, bf16[3,512,512]{2,1,0:T(8,128)(2,1)S(1)}, u32[]{:S(2)}, u32[]{:S(2)}) collective-permute-start(bf16[3,512,512]{2,1,0:T(8,128)(2,1)S(1)} %shard_map.85), channel_id=1, source_target_pairs={{0,4},{4,0},{1,5},{5,1},{2,6},{6,2},{3,7},{7,3},{8,12},{12,8},{9,1... | collective-permute-start | bytes 4718600 | tf_op jit(solution)/shard_map/ppermute | solution.py:188
  6.2 3.0 %collective-permute-done.got_ref = bf16[3,512,512]{2,1,0:T(8,128)(2,1)S(1)} collective-permute-done((bf16[3,512,512]{2,1,0:T(8,128)(2,1)S(1)}, bf16[3,512,512]{2,1,0:T(8,128)(2,1)S(1)}, u32[]{:S(2)}, u32[]{:S(2)}) %collective-permute-start) | collective-permute-done | bytes 1572896 | tf_op jit(solution)/shard_map/ppermute | solution.py:188
  9.2 0.9 shard_map.86
  10.1 17.7 %all_to_all.30.terms_ref = bf16[4,24,16,512]{3,2,1,0:T(8,128)(2,1)S(1)} all-to-all(bf16[4,24,16,512]{3,2,1,0:T(8,128)(2,1)S(1)} %bitcast.34), channel_id=1, replica_groups={{0,24,96,120},{48,72,144,168},{192,216,288,312},{240,264,336,360},{384,..., dimensions={0} | all-to-all | bytes 3145728 | tf_op jit(solution)/shard_map/all_to_all | solution.py:171
  27.8 0.2 shard_map.87
  28.1 0.0 copy-start.1
  28.1 0.0 copy-start.2
  28.1 23.2 %all_to_all.31.terms_ref = bf16[24,16,512]{2,1,0:T(8,128)(2,1)S(1)} all-to-all(bf16[24,16,512]{2,1,0:T(8,128)(2,1)S(1)} %shard_map.87), channel_id=1, replica_groups={{0,8,16,48,56,64,192,200,208,240,248,256,384,392,400,432,440,448,576,58..., dimensions={0} | all-to-all | bytes 786432 | tf_op jit(solution)/shard_map/all_to_all | solution.py:171
  51.3 0.1 shard_map.88
  51.4 13.7 %all_to_all.32 = bf16[8,16,512]{2,1,0:T(8,128)(2,1)S(1)} all-to-all(bf16[8,16,512]{2,1,0:T(8,128)(2,1)S(1)} %shard_map.88), channel_id=1, replica_groups={{0,48,192,240,384,432,576,624},{24,72,216,264,408,456,600,648},{96,144,..., dimensions={0} | all-to-all | bytes 262144 | tf_op jit(solution)/shard_map/all_to_all | solution.py:171
  65.1 10.6 %all_to_all.33 = bf16[4,128,512]{2,1,0:T(8,128)(2,1)S(1)} all-to-all(bf16[4,128,512]{2,1,0:T(8,128)(2,1)S(1)} %shard_map.89), channel_id=1, replica_groups={{0,24,96,120},{48,72,144,168},{192,216,288,312},{240,264,336,360},{384,..., dimensions={0} | all-to-all | bytes 1048576 | tf_op jit(solution)/shard_map/all_to_all | solution.py:171
  75.7 2.0 %shard_map.90 = (bf16[4,128,512]{2,1,0:T(8,128)(2,1)S(1)}, bf16[3,128,512]{2,1,0:T(8,128)(2,1)S(1)}) custom-call(s32[3]{0:T(128)S(1)} %pad_add_fusion.place_ref, bf16[512,512]{1,0:T(8,128)(2,1)S(1)} %bitcast.36, bf16[512,512]{1,0:T(8,128)(2,1)S(1)} %bitcast.30, bf16[512,512]{1,0:T(8,128)(2,1)S(1)} %bitcast.37), custom_call_target="tpu_custom_call" | custom-call | bytes 2097152 | tf_op jit(solution)/shard_map/pallas_call | solution.py:47
  77.8 11.7 %all_to_all.34.strips_ref = bf16[3,128,512]{2,1,0:T(8,128)(2,1)S(1)} all-to-all(bf16[3,128,512]{2,1,0:T(8,128)(2,1)S(1)} %get-tuple-element.5), channel_id=1, replica_groups=mesh['y'=8,'x'=4,'zl'=3,'core'=2,'tensor'=4] {'zl'}, dimensions={0} | all-to-all | bytes 786432 | tf_op jit(solution)/shard_map/all_to_all | solution.py:206
  89.4 0.6 shard_map.91
  90.1 16.2 %all_to_all.35.refs_0_ = bf16[4,2,128,512]{3,2,1,0:T(8,128)(2,1)S(1)} all-to-all(bf16[4,2,128,512]{3,2,1,0:T(8,128)(2,1)S(1)} %shard_map.91), channel_id=1, replica_groups={{0,24,96,120},{48,72,144,168},{192,216,288,312},{240,264,336,360},{384,..., dimensions={0} | all-to-all | bytes 2097152 | tf_op jit(solution)/shard_map/all_to_all | solution.py:171
  106.3 3.6 %collective-permute-start.1 = (bf16[4,2,128,512]{3,2,1,0:T(8,128)(2,1)S(1)}, bf16[4,2,128,512]{3,2,1,0:T(8,128)(2,1)S(1)}, u32[]{:S(2)}, u32[]{:S(2)}) collective-permute-start(bf16[4,2,128,512]{3,2,1,0:T(8,128)(2,1)S(1)} %all_to_all.35.refs_0_), channel_id=1, source_target_pairs={{0,4},{4,0},{1,5},{5,1},{2,6},{6,2},{3,7},{7,3},{8,12},{12,8},{9,1... | collective-permute-start | bytes 3145736 | tf_op jit(solution)/shard_map/ppermute | solution.py:210
  109.9 2.1 %collective-permute-start.2 = (bf16[4,128,512]{2,1,0:T(8,128)(2,1)S(1)}, bf16[4,128,512]{2,1,0:T(8,128)(2,1)S(1)}, u32[]{:S(2)}, u32[]{:S(2)}) collective-permute-start(bf16[4,128,512]{2,1,0:T(8,128)(2,1)S(1)} %get-tuple-element.6.refs_0_), channel_id=1, source_target_pairs={{0,4},{4,0},{1,5},{5,1},{2,6},{6,2},{3,7},{7,3},{8,12},{12,8},{9,1... | collective-permute-start | bytes 1572872 | tf_op jit(solution)/shard_map/ppermute | solution.py:205
  112.0 1.4 %fusion.4 = f32[1,1,512,512]{3,2,1,0:T(8,128)} fusion(bf16[512,512]{1,0:T(8,128)(2,1)S(1)} %bitcast.31, f32[1,1,512,512]{3,2,1,0:T(8,128)S(1)} %copy-done.5), kind=kOutput, calls=%fused_computation.6 | convolution fusion | flops 269221888 | bytes 2621440 | tf_op jit(solution)/shard_map/dot_general | solution.py:214
  113.4 1.5 %fusion.2 = f32[1,1,512,512]{3,2,1,0:T(8,128)} fusion(bf16[4,128,512]{2,1,0:T(8,128)(2,1)S(1)} %all_to_all.33, f32[1,1,512,512]{3,2,1,0:T(8,128)S(1)} %copy-done.6), kind=kOutput, calls=%fused_computation.3 | convolution fusion | flops 269221888 | bytes 2621440 | tf_op jit(solution)/shard_map/dot_general | solution.py:218
  114.9 1.5 %place.2.refs_2_ = bf16[6,4,128,512]{3,2,1,0:T(8,128)(2,1)} custom-call(s32[1,6]{1,0:T(1,128)S(1)} %copy-done.4, s32[3]{0:T(128)S(1)} %pad_add_fusion.place_ref, bf16[4,128,512]{2,1,0:T(8,128)(2,1)S(1)} %get-tuple-element.6.refs_0_, bf16[4,128,512]{2,1,0:T(8,128)(2,1)S(1)} %collective-permute-done.2.refs_1_), custom_call_target="tpu_custom_call" | custom-call | bytes 1048576 | tf_op jit(solution)/shard_map/place/pallas_call | solution.py:155
  116.4 1.9 %place.3 = bf16[6,4,128,512]{3,2,1,0:T(8,128)(2,1)} custom-call(s32[1,6]{1,0:T(1,128)S(1)} %copy-done.4, s32[3]{0:T(128)S(1)} %pad_add_fusion.place_ref, bf16[4,2,128,512]{3,2,1,0:T(8,128)(2,1)S(1)} %all_to_all.35.refs_0_, bf16[4,2,128,512]{3,2,1,0:T(8,128)(2,1)S(1)} %collective-permute-done.1.refs_1_, ...), custom_call_target="tpu_custom_call", output_to_operand_aliasing={{}: (4, {})} | custom-call | bytes 2097152 | tf_op jit(solution)/shard_map/place/pallas_call | solution.py:155
  (14 shorter events, 0.1 us)
Async XLA Ops:
  0.7 0.7 copy-start.3
  1.4 7.8 %copy-start = (bf16[1,6,512,512]{3,2,1,0:T(8,128)(2,1)S(1)}, bf16[1,6,512,512]{3,2,1,0:T(8,128)(2,1)}, u32[]{:S(2)}) copy-start(bf16[1,6,512,512]{3,2,1,0:T(8,128)(2,1)} %param.6) | copy-start | bytes 9437188
  3.6 5.6 %collective-permute-start = (bf16[3,512,512]{2,1,0:T(8,128)(2,1)S(1)}, bf16[3,512,512]{2,1,0:T(8,128)(2,1)S(1)}, u32[]{:S(2)}, u32[]{:S(2)}) collective-permute-start(bf16[3,512,512]{2,1,0:T(8,128)(2,1)S(1)} %shard_map.85), channel_id=1, source_target_pairs={{0,4},{4,0},{1,5},{5,1},{2,6},{6,2},{3,7},{7,3},{8,12},{12,8},{9,1... | collective-permute-start | bytes 4718600 | tf_op jit(solution)/shard_map/ppermute | solution.py:188
  28.1 47.7 %copy-start.1 = (bf16[1,1,512,512]{3,2,1,0:T(8,128)(2,1)S(1)}, bf16[1,1,512,512]{3,2,1,0:T(8,128)(2,1)}, u32[]{:S(2)}) copy-start(bf16[1,1,512,512]{3,2,1,0:T(8,128)(2,1)} %param.10) | copy-start | bytes 1572868
  28.1 47.7 %copy-start.2 = (bf16[1,1,512,512]{3,2,1,0:T(8,128)(2,1)S(1)}, bf16[1,1,512,512]{3,2,1,0:T(8,128)(2,1)}, u32[]{:S(2)}) copy-start(bf16[1,1,512,512]{3,2,1,0:T(8,128)(2,1)} %param.11) | copy-start | bytes 1572868
  89.4 22.5 %copy-start.5 = (f32[1,1,512,512]{3,2,1,0:T(8,128)S(1)}, f32[1,1,512,512]{3,2,1,0:T(8,128)}, u32[]{:S(2)}) copy-start(f32[1,1,512,512]{3,2,1,0:T(8,128)} %param.8) | copy-start | bytes 3145732
  106.3 10.1 %collective-permute-start.1 = (bf16[4,2,128,512]{3,2,1,0:T(8,128)(2,1)S(1)}, bf16[4,2,128,512]{3,2,1,0:T(8,128)(2,1)S(1)}, u32[]{:S(2)}, u32[]{:S(2)}) collective-permute-start(bf16[4,2,128,512]{3,2,1,0:T(8,128)(2,1)S(1)} %all_to_all.35.refs_0_), channel_id=1, source_target_pairs={{0,4},{4,0},{1,5},{5,1},{2,6},{6,2},{3,7},{7,3},{8,12},{12,8},{9,1... | collective-permute-start | bytes 3145736 | tf_op jit(solution)/shard_map/ppermute | solution.py:210
  109.9 3.5 %copy-start.6 = (f32[1,1,512,512]{3,2,1,0:T(8,128)S(1)}, f32[1,1,512,512]{3,2,1,0:T(8,128)}, u32[]{:S(2)}) copy-start(f32[1,1,512,512]{3,2,1,0:T(8,128)} %param.9) | copy-start | bytes 3145732
  109.9 5.0 %collective-permute-start.2 = (bf16[4,128,512]{2,1,0:T(8,128)(2,1)S(1)}, bf16[4,128,512]{2,1,0:T(8,128)(2,1)S(1)}, u32[]{:S(2)}, u32[]{:S(2)}) collective-permute-start(bf16[4,128,512]{2,1,0:T(8,128)(2,1)S(1)} %get-tuple-element.6.refs_0_), channel_id=1, source_target_pairs={{0,4},{4,0},{1,5},{5,1},{2,6},{6,2},{3,7},{7,3},{8,12},{12,8},{9,1... | collective-permute-start | bytes 1572872 | tf_op jit(solution)/shard_map/ppermute | solution.py:205
  113.4 1.5 %copy-start.4 = (s32[1,6]{1,0:T(1,128)S(1)}, s32[1,6]{1,0:T(1,128)}, u32[]{:S(2)}) copy-start(s32[1,6]{1,0:T(1,128)} %table_ref.7) | copy-start | bytes 76

commit v2 on v1

--- a/solution.py
+++ b/solution.py
@@ -29,7 +29,9 @@
 
 
 QUADS = [[device(c, z, f, q) for q in range(NEAR)] for c in range(NC) for z in range(NZ) for f in range(AWAY)]
-AWAYS = [[device(c, z, f, q) for f in range(AWAY)] for c in range(NC) for z in range(NZ) for q in range(NEAR)]
+PLANES = [
+    [device(c, z, f, q) for q in range(NEAR) for f in range(AWAY)] for c in range(NC) for z in range(NZ)
+]
 AWAY_Z = [
     [device(c, z, f, q) for f in range(AWAY) for z in range(NZ)] for c in range(NC) for q in range(NEAR)
 ]
@@ -102,11 +104,6 @@
     strip = total.astype(out_ref.dtype)
     for i in range(out_ref.shape[0]):
         out_ref[i] = strip
-
-
-def repeat_kernel(strip_ref, out_ref):
-    for i in range(out_ref.shape[0]):
-        out_ref[i] = strip_ref[...]
 
 
 def foreign_kernel(place_ref, strips_ref, out_ref):
@@ -189,10 +186,8 @@
     pieces = call(pair_kernel, (NEAR, AWAY, NZ, ROWS, B), (owner_table, here), (grad_partial[0], got), cost=2**22)
     in_quad = exchange(pieces.reshape(NEAR, AWAY * NZ, ROWS, B), QUADS)
     part = call(sum_kernel, (AWAY * NZ, ROWS, B), (), (in_quad,), cost=2**21)
-    strips = call(spread_kernel, (AWAY, ROWS, B), (), (exchange(part, AWAY_Z),), cost=2**20)
-    strip = exchange(strips, AWAYS).reshape(B // NEAR, B)
-    strips = call(repeat_kernel, (NEAR, B // NEAR, B), (), (strip,), cost=2**20)
-    owned = exchange(strips, QUADS).reshape(B, B)
+    strips = call(spread_kernel, (NEAR * AWAY, ROWS, B), (), (exchange(part, AWAY_Z),), cost=2**20)
+    owned = exchange(strips, PLANES).reshape(B, B)
 
     scaled, strips = call(
         direction_kernel,
@@ -204,9 +199,9 @@
     )
     scaled_other = lax.ppermute(scaled, "core", SWAP)
     strips = lax.all_to_all(strips, "zl", 0, 0)
+    direction = place(owner_table, here, [(0, 0, 0), (1, 0, 1)], [scaled, scaled_other])
     foreign = call(foreign_kernel, (NEAR, NZ - 1, B // NEAR, B), (here,), (strips,), cost=2**20)
     foreign = exchange(foreign, QUADS)
-    direction = place(owner_table, here, [(0, 0, 0), (1, 0, 1)], [scaled, scaled_other])
     foreign_other = lax.ppermute(foreign, "core", SWAP)
     late = [(0, 1, 0), (0, 2, 0), (1, 1, 1), (1, 2, 1)]
     direction = place(owner_table, here, late, [foreign, foreign_other], direction).reshape(NZ * NC, B, B)

time: 119 us -> 118 us (level)
  the two profiles are of different devices: /device:TPU:193 before, /device:TPU:1 now
where the time goes in v2:
time: 118 us; the launch traced here: 116 us
  blocking collectives  79.4 us (67%)
  starting transfers between devices  19.1 us (16%)
  Pallas kernels  9.52 us (8%)
  waiting for transfers between devices  3.02 us (3%)
  matrix products  2.89 us (2%)
    all_to_all x4, blocking collectives, exchange(): return lax.all_to_all(pieces, SLAB, 0, 0, axis_index_groups=groups)  70.3 us
    ppermute x1, starting transfers between devices, step(): got = lax.ppermute(give, 'core', SWAP)  12.4 us
    all_to_all x1, blocking collectives, step(): strips = lax.all_to_all(strips, 'zl', 0, 0)  9.11 us
    pallas_call x6, Pallas kernels, call(): pl.pallas_call(kernel, out_shape=tuple((pltpu.VMEM(o, jnp.bfloat16) for o...  6.07 us
    ppermute x1, starting transfers between devices, step(): foreign_other = lax.ppermute(foreign, 'core', SWAP)  4.7 us
    pallas_call x2, Pallas kernels, place(): pl.pallas_call(functools.partial(place_kernel, parts), out_shape=jax.Shap...  3.45 us
    ppermute x1, waiting for transfers between devices, step(): got = lax.ppermute(give, 'core', SWAP)  3.01 us
  transfers between devices with their start and end apart: 3, of which 1 were waited for; matrix products, arithmetic and copies ran while one was open for 3% of the time, Pallas kernels for 1%

profile of v2, /device:TPU:1, one launch (start us, length us, event | category | flops | bytes accessed | tf_op | source)
XLA Modules:
  0.0 115.6 jit_solution(5497065727490629495)
XLA Ops:
  0.7 0.1 pad_add_fusion.place_ref
  0.7 0.7 copy-done.3
  1.4 2.2 %shard_map.85 = bf16[3,512,512]{2,1,0:T(8,128)(2,1)S(1)} custom-call(s32[1,6]{1,0:T(1,128)S(1)} %copy-done.3, s32[3]{0:T(128)S(1)} %pad_add_fusion.place_ref, bf16[6,512,512]{2,1,0:T(8,128)(2,1)} %bitcast.29), custom_call_target="tpu_custom_call" | custom-call | bytes 2097152 | tf_op jit(solution)/shard_map/pallas_call | solution.py:49
  3.6 12.4 %collective-permute-start = (bf16[3,512,512]{2,1,0:T(8,128)(2,1)S(1)}, bf16[3,512,512]{2,1,0:T(8,128)(2,1)S(1)}, u32[]{:S(2)}, u32[]{:S(2)}) collective-permute-start(bf16[3,512,512]{2,1,0:T(8,128)(2,1)S(1)} %shard_map.85), channel_id=1, source_target_pairs={{0,4},{4,0},{1,5},{5,1},{2,6},{6,2},{3,7},{7,3},{8,12},{12,8},{9,1... | collective-permute-start | bytes 4718600 | tf_op jit(solution)/shard_map/ppermute | solution.py:185
  16.0 3.0 %collective-permute-done.got_ref = bf16[3,512,512]{2,1,0:T(8,128)(2,1)S(1)} collective-permute-done((bf16[3,512,512]{2,1,0:T(8,128)(2,1)S(1)}, bf16[3,512,512]{2,1,0:T(8,128)(2,1)S(1)}, u32[]{:S(2)}, u32[]{:S(2)}) %collective-permute-start) | collective-permute-done | bytes 1572896 | tf_op jit(solution)/shard_map/ppermute | solution.py:185
  19.0 0.9 shard_map.86
  19.9 15.7 %all_to_all.25.terms_ref = bf16[4,24,16,512]{3,2,1,0:T(8,128)(2,1)S(1)} all-to-all(bf16[4,24,16,512]{3,2,1,0:T(8,128)(2,1)S(1)} %bitcast.33), channel_id=1, replica_groups={{0,24,96,120},{48,72,144,168},{192,216,288,312},{240,264,336,360},{384,..., dimensions={0} | all-to-all | bytes 3145728 | tf_op jit(solution)/shard_map/all_to_all | solution.py:168
  35.7 0.2 shard_map.87
  35.9 0.0 copy-start.1
  35.9 0.0 copy-start.2
  35.9 17.2 %all_to_all.26.terms_ref = bf16[24,16,512]{2,1,0:T(8,128)(2,1)S(1)} all-to-all(bf16[24,16,512]{2,1,0:T(8,128)(2,1)S(1)} %shard_map.87), channel_id=1, replica_groups={{0,8,16,48,56,64,192,200,208,240,248,256,384,392,400,432,440,448,576,58..., dimensions={0} | all-to-all | bytes 786432 | tf_op jit(solution)/shard_map/all_to_all | solution.py:168
  53.1 0.1 shard_map.88
  53.2 24.4 %all_to_all.27 = bf16[32,16,512]{2,1,0:T(8,128)(2,1)S(1)} all-to-all(bf16[32,16,512]{2,1,0:T(8,128)(2,1)S(1)} %shard_map.88), channel_id=1, replica_groups={{0,48,192,240,384,432,576,624,24,72,216,264,408,456,600,648,96,144,288,..., dimensions={0} | all-to-all | bytes 1048576 | tf_op jit(solution)/shard_map/all_to_all | solution.py:168
  77.6 2.0 %shard_map.89 = (bf16[4,128,512]{2,1,0:T(8,128)(2,1)S(1)}, bf16[3,128,512]{2,1,0:T(8,128)(2,1)S(1)}) custom-call(s32[3]{0:T(128)S(1)} %pad_add_fusion.place_ref, bf16[512,512]{1,0:T(8,128)(2,1)S(1)} %bitcast.34, bf16[512,512]{1,0:T(8,128)(2,1)S(1)} %bitcast.31, bf16[512,512]{1,0:T(8,128)(2,1)S(1)} %bitcast.35), custom_call_target="tpu_custom_call" | custom-call | bytes 2097152 | tf_op jit(solution)/shard_map/pallas_call | solution.py:49
  79.6 9.1 %all_to_all.28.strips_ref = bf16[3,128,512]{2,1,0:T(8,128)(2,1)S(1)} all-to-all(bf16[3,128,512]{2,1,0:T(8,128)(2,1)S(1)} %get-tuple-element.5), channel_id=1, replica_groups=mesh['y'=8,'x'=4,'zl'=3,'core'=2,'tensor'=4] {'zl'}, dimensions={0} | all-to-all | bytes 786432 | tf_op jit(solution)/shard_map/all_to_all | solution.py:201
  88.7 0.6 shard_map.90
  89.3 13.1 %all_to_all.29.refs_0_ = bf16[4,2,128,512]{3,2,1,0:T(8,128)(2,1)S(1)} all-to-all(bf16[4,2,128,512]{3,2,1,0:T(8,128)(2,1)S(1)} %shard_map.90), channel_id=1, replica_groups={{0,24,96,120},{48,72,144,168},{192,216,288,312},{240,264,336,360},{384,..., dimensions={0} | all-to-all | bytes 2097152 | tf_op jit(solution)/shard_map/all_to_all | solution.py:168
  102.4 4.7 %collective-permute-start.1 = (bf16[4,2,128,512]{3,2,1,0:T(8,128)(2,1)S(1)}, bf16[4,2,128,512]{3,2,1,0:T(8,128)(2,1)S(1)}, u32[]{:S(2)}, u32[]{:S(2)}) collective-permute-start(bf16[4,2,128,512]{3,2,1,0:T(8,128)(2,1)S(1)} %all_to_all.29.refs_0_), channel_id=1, source_target_pairs={{0,4},{4,0},{1,5},{5,1},{2,6},{6,2},{3,7},{7,3},{8,12},{12,8},{9,1... | collective-permute-start | bytes 3145736 | tf_op jit(solution)/shard_map/ppermute | solution.py:205
  107.1 0.0 copy-start.6
  107.1 2.1 %collective-permute-start.2 = (bf16[4,128,512]{2,1,0:T(8,128)(2,1)S(1)}, bf16[4,128,512]{2,1,0:T(8,128)(2,1)S(1)}, u32[]{:S(2)}, u32[]{:S(2)}) collective-permute-start(bf16[4,128,512]{2,1,0:T(8,128)(2,1)S(1)} %get-tuple-element.6.refs_0_), channel_id=1, source_target_pairs={{0,4},{4,0},{1,5},{5,1},{2,6},{6,2},{3,7},{7,3},{8,12},{12,8},{9,1... | collective-permute-start | bytes 1572872 | tf_op jit(solution)/shard_map/ppermute | solution.py:200
  109.2 1.4 %fusion.2 = f32[1,1,512,512]{3,2,1,0:T(8,128)} fusion(bf16[512,512]{1,0:T(8,128)(2,1)S(1)} %bitcast.32, f32[1,1,512,512]{3,2,1,0:T(8,128)S(1)} %copy-done.5), kind=kOutput, calls=%fused_computation.4 | convolution fusion | flops 269221888 | bytes 2621440 | tf_op jit(solution)/shard_map/dot_general | solution.py:209
  110.6 1.5 %fusion.4 = f32[1,1,512,512]{3,2,1,0:T(8,128)} fusion(bf16[32,16,512]{2,1,0:T(8,128)(2,1)S(1)} %all_to_all.27, f32[1,1,512,512]{3,2,1,0:T(8,128)S(1)} %copy-done.6), kind=kOutput, calls=%fused_computation.6 | convolution fusion | flops 269221888 | bytes 2621440 | tf_op jit(solution)/shard_map/dot_general | solution.py:213
  112.1 1.5 %place.2.refs_2_ = bf16[6,4,128,512]{3,2,1,0:T(8,128)(2,1)} custom-call(s32[1,6]{1,0:T(1,128)S(1)} %copy-done.4, s32[3]{0:T(128)S(1)} %pad_add_fusion.place_ref, bf16[4,128,512]{2,1,0:T(8,128)(2,1)S(1)} %get-tuple-element.6.refs_0_, bf16[4,128,512]{2,1,0:T(8,128)(2,1)S(1)} %collective-permute-done.2.refs_1_), custom_call_target="tpu_custom_call" | custom-call | bytes 1048576 | tf_op jit(solution)/shard_map/place/pallas_call | solution.py:152
  113.6 1.9 %place.3 = bf16[6,4,128,512]{3,2,1,0:T(8,128)(2,1)} custom-call(s32[1,6]{1,0:T(1,128)S(1)} %copy-done.4, s32[3]{0:T(128)S(1)} %pad_add_fusion.place_ref, bf16[4,2,128,512]{3,2,1,0:T(8,128)(2,1)S(1)} %all_to_all.29.refs_0_, bf16[4,2,128,512]{3,2,1,0:T(8,128)(2,1)S(1)} %collective-permute-done.1.refs_1_, ...), custom_call_target="tpu_custom_call", output_to_operand_aliasing={{}: (4, {})} | custom-call | bytes 2097152 | tf_op jit(solution)/shard_map/place/pallas_call | solution.py:152
  (12 shorter events, 0.0 us)
Async XLA Ops:
  0.7 0.7 copy-start.3
  1.4 17.6 %copy-start = (bf16[1,6,512,512]{3,2,1,0:T(8,128)(2,1)S(1)}, bf16[1,6,512,512]{3,2,1,0:T(8,128)(2,1)}, u32[]{:S(2)}) copy-start(bf16[1,6,512,512]{3,2,1,0:T(8,128)(2,1)} %param.6) | copy-start | bytes 9437188
  3.6 15.4 %collective-permute-start = (bf16[3,512,512]{2,1,0:T(8,128)(2,1)S(1)}, bf16[3,512,512]{2,1,0:T(8,128)(2,1)S(1)}, u32[]{:S(2)}, u32[]{:S(2)}) collective-permute-start(bf16[3,512,512]{2,1,0:T(8,128)(2,1)S(1)} %shard_map.85), channel_id=1, source_target_pairs={{0,4},{4,0},{1,5},{5,1},{2,6},{6,2},{3,7},{7,3},{8,12},{12,8},{9,1... | collective-permute-start | bytes 4718600 | tf_op jit(solution)/shard_map/ppermute | solution.py:185
  35.9 41.7 %copy-start.1 = (bf16[1,1,512,512]{3,2,1,0:T(8,128)(2,1)S(1)}, bf16[1,1,512,512]{3,2,1,0:T(8,128)(2,1)}, u32[]{:S(2)}) copy-start(bf16[1,1,512,512]{3,2,1,0:T(8,128)(2,1)} %param.10) | copy-start | bytes 1572868
  35.9 41.7 %copy-start.2 = (bf16[1,1,512,512]{3,2,1,0:T(8,128)(2,1)S(1)}, bf16[1,1,512,512]{3,2,1,0:T(8,128)(2,1)}, u32[]{:S(2)}) copy-start(bf16[1,1,512,512]{3,2,1,0:T(8,128)(2,1)} %param.11) | copy-start | bytes 1572868
  88.7 20.5 %copy-start.5 = (f32[1,1,512,512]{3,2,1,0:T(8,128)S(1)}, f32[1,1,512,512]{3,2,1,0:T(8,128)}, u32[]{:S(2)}) copy-start(f32[1,1,512,512]{3,2,1,0:T(8,128)} %param.8) | copy-start | bytes 3145732
  102.4 11.2 %collective-permute-start.1 = (bf16[4,2,128,512]{3,2,1,0:T(8,128)(2,1)S(1)}, bf16[4,2,128,512]{3,2,1,0:T(8,128)(2,1)S(1)}, u32[]{:S(2)}, u32[]{:S(2)}) collective-permute-start(bf16[4,2,128,512]{3,2,1,0:T(8,128)(2,1)S(1)} %all_to_all.29.refs_0_), channel_id=1, source_target_pairs={{0,4},{4,0},{1,5},{5,1},{2,6},{6,2},{3,7},{7,3},{8,12},{12,8},{9,1... | collective-permute-start | bytes 3145736 | tf_op jit(solution)/shard_map/ppermute | solution.py:205
  107.1 3.5 %copy-start.6 = (f32[1,1,512,512]{3,2,1,0:T(8,128)S(1)}, f32[1,1,512,512]{3,2,1,0:T(8,128)}, u32[]{:S(2)}) copy-start(f32[1,1,512,512]{3,2,1,0:T(8,128)} %param.9) | copy-start | bytes 3145732
  107.1 5.0 %collective-permute-start.2 = (bf16[4,128,512]{2,1,0:T(8,128)(2,1)S(1)}, bf16[4,128,512]{2,1,0:T(8,128)(2,1)S(1)}, u32[]{:S(2)}, u32[]{:S(2)}) collective-permute-start(bf16[4,128,512]{2,1,0:T(8,128)(2,1)S(1)} %get-tuple-element.6.refs_0_), channel_id=1, source_target_pairs={{0,4},{4,0},{1,5},{5,1},{2,6},{6,2},{3,7},{7,3},{8,12},{12,8},{9,1... | collective-permute-start | bytes 1572872 | tf_op jit(solution)/shard_map/ppermute | solution.py:200
  110.6 1.5 %copy-start.4 = (s32[1,6]{1,0:T(1,128)S(1)}, s32[1,6]{1,0:T(1,128)}, u32[]{:S(2)}) copy-start(s32[1,6]{1,0:T(1,128)} %table_ref.7) | copy-start | bytes 76

commit v3 on v2

--- a/solution.py
+++ b/solution.py
@@ -29,18 +29,15 @@
 
 
 QUADS = [[device(c, z, f, q) for q in range(NEAR)] for c in range(NC) for z in range(NZ) for f in range(AWAY)]
-PLANES = [
-    [device(c, z, f, q) for q in range(NEAR) for f in range(AWAY)] for c in range(NC) for z in range(NZ)
-]
 AWAY_Z = [
     [device(c, z, f, q) for f in range(AWAY) for z in range(NZ)] for c in range(NC) for q in range(NEAR)
 ]
 
 
-def block_of(table_ref, owner):
+def block_of(info_ref, owner):
     found = jnp.int32(0)
     for k in range(NZ * NC):
-        found = jnp.where(table_ref[0, k] == owner, jnp.int32(k), found)
+        found = jnp.where(info_ref[3 + k] == owner, jnp.int32(k), found)
     return found
 
 
@@ -62,11 +59,10 @@
     )(*scalars, *held)
 
 
-def give_kernel(table_ref, place_ref, grad_ref, out_ref, sem):
+def fetch_kernel(other, info_ref, grad_ref, out_ref, sem):
+    core = 1 - info_ref[0] if other else info_ref[0]
     copies = [
-        pltpu.make_async_copy(
-            grad_ref.at[block_of(table_ref, 2 * z + 1 - place_ref[0])], out_ref.at[z], sem.at[z]
-        )
+        pltpu.make_async_copy(grad_ref.at[block_of(info_ref, 2 * z + core)], out_ref.at[z], sem.at[z])
         for z in range(NZ)
     ]
     for copy in copies:
@@ -75,13 +71,17 @@
         copy.wait()
 
 
-def pair_kernel(table_ref, place_ref, grad_ref, got_ref, out_ref):
-    for z in range(NZ):
-        mine = block_of(table_ref, 2 * z + place_ref[0])
-        for piece in range(NX * NY):
-            rows = pl.ds(piece * ROWS, ROWS)
-            total = grad_ref[mine, rows].astype(jnp.float32) + got_ref[z, rows].astype(jnp.float32)
-            out_ref[piece // AWAY, piece % AWAY, z] = total.astype(out_ref.dtype)
+def pair_kernel(info_ref, keep_ref, got_ref, out_ref):
+    core = info_ref[0]
+    for y in range(NY):
+        for x in range(NX):
+            up, right = lax.rem(y + NY - core, jnp.int32(NY)), lax.rem(x + NX - core, jnp.int32(NX))
+            member = 2 * lax.rem(up, jnp.int32(2)) + lax.rem(right, jnp.int32(2))
+            quad = 2 * (up >> 1) + (right >> 1)
+            rows = pl.ds((y * NX + x) * ROWS, ROWS)
+            for z in range(NZ):
+                total = keep_ref[z, rows].astype(jnp.float32) + got_ref[z, rows].astype(jnp.float32)
+                out_ref[member, quad, z] = total.astype(out_ref.dtype)
 
 
 def sum_kernel(terms_ref, out_ref):
@@ -106,14 +106,14 @@
         out_ref[i] = strip
 
 
-def foreign_kernel(place_ref, strips_ref, out_ref):
+def foreign_kernel(info_ref, strips_ref, out_ref):
     for d in range(1, NZ):
-        strip = strips_ref[lax.rem(place_ref[1] + NZ - d, jnp.int32(NZ))]
+        strip = strips_ref[lax.rem(info_ref[1] + NZ - d, jnp.int32(NZ))]
         for i in range(out_ref.shape[0]):
             out_ref[i, d - 1] = strip
 
 
-def direction_kernel(place_ref, left_ref, owned_ref, right_ref, out_ref, strips_ref, full_ref):
+def direction_kernel(info_ref, left_ref, owned_ref, right_ref, out_ref, strips_ref, full_ref):
     step = B // NEAR
     square = jnp.zeros((8, 128), jnp.float32)
     for i in range(NEAR):
@@ -125,19 +125,19 @@
     scale = lax.rsqrt(jnp.sum(square) * (1.0 / (B * B)) + epsilon)
     for i in range(NEAR):
         out_ref[i] = (full_ref[i] * scale).astype(out_ref.dtype)
-    strip = out_ref[place_ref[2]]
+    strip = out_ref[info_ref[2]]
     for z in range(NZ):
         strips_ref[z] = strip
 
 
-def place_kernel(parts, table_ref, place_ref, *refs):
+def place_kernel(parts, info_ref, *refs):
     out_ref, sem = refs[-2], refs[-1]
     copies = []
     for n, (i, d, s) in enumerate(parts):
-        core = place_ref[0] if s == 0 else 1 - place_ref[0]
-        z = lax.rem(place_ref[1] + NZ - d, jnp.int32(NZ))
+        core = info_ref[0] if s == 0 else 1 - info_ref[0]
+        z = lax.rem(info_ref[1] + NZ - d, jnp.int32(NZ))
         block = refs[i] if d == 0 else refs[i].at[:, d - 1]
-        to = out_ref.at[block_of(table_ref, 2 * z + core)]
+        to = out_ref.at[block_of(info_ref, 2 * z + core)]
         copies.append(pltpu.make_async_copy(block, to, sem.at[n]))
     for copy in copies:
         copy.start()
@@ -145,23 +145,23 @@
         copy.wait()
 
 
-def place(table, here, parts, arrays, into=None):
+def place(info, parts, arrays, into=None):
     count = len(arrays)
     extra = [] if into is None else [into]
     held = [pltpu.with_memory_space_constraint(a, VMEM) for a in arrays]
     return pl.pallas_call(
         functools.partial(place_kernel, parts),
         out_shape=jax.ShapeDtypeStruct((NZ * NC, NEAR, B // NEAR, B), jnp.bfloat16),
-        in_specs=[pl.BlockSpec(memory_space=SMEM)] * 2
+        in_specs=[pl.BlockSpec(memory_space=SMEM)]
         + [pl.BlockSpec(memory_space=VMEM)] * count
         + [pl.BlockSpec(memory_space=pl.ANY)] * len(extra),
         out_specs=pl.BlockSpec(memory_space=pl.ANY),
         scratch_shapes=[pltpu.SemaphoreType.DMA((len(parts),))],
-        input_output_aliases={2 + count: 0} if extra else {},
+        input_output_aliases={1 + count: 0} if extra else {},
         compiler_params=pltpu.CompilerParams(vmem_limit_bytes=2**22),
         cost_estimate=pl.CostEstimate(flops=0, bytes_accessed=2 * len(parts) * B * B, transcendentals=0),
         name="place",
-    )(table, here, *held, *extra)
+    )(info, *held, *extra)
 
 
 def exchange(pieces, groups):
@@ -172,39 +172,44 @@
     core = lax.axis_index("core")
     quarter = 2 * ((lax.axis_index("y") + core) % 2) + (lax.axis_index("x") + core) % 2
     here = jnp.stack([core, lax.axis_index("zl"), quarter]).astype(jnp.int32)
-
-    give = call(
-        give_kernel,
-        (NZ, B, B),
-        (owner_table, here),
-        (grad_partial[0],),
-        scratch=[pltpu.SemaphoreType.DMA((NZ,))],
-        cost=2**21,
-        space=HBM,
-    )
+    info = jnp.concatenate([here, owner_table[0]])
+
+    def fetch(other):
+        return call(
+            functools.partial(fetch_kernel, other),
+            (NZ, B, B),
+            (info,),
+            (grad_partial[0],),
+            scratch=[pltpu.SemaphoreType.DMA((NZ,))],
+            cost=2**21,
+            space=HBM,
+        )
+
+    give = fetch(True)
     got = lax.ppermute(give, "core", SWAP)
-    pieces = call(pair_kernel, (NEAR, AWAY, NZ, ROWS, B), (owner_table, here), (grad_partial[0], got), cost=2**22)
+    keep = fetch(False)
+    pieces = call(pair_kernel, (NEAR, AWAY, NZ, ROWS, B), (info,), (keep, got), cost=2**22)
     in_quad = exchange(pieces.reshape(NEAR, AWAY * NZ, ROWS, B), QUADS)
     part = call(sum_kernel, (AWAY * NZ, ROWS, B), (), (in_quad,), cost=2**21)
     strips = call(spread_kernel, (NEAR * AWAY, ROWS, B), (), (exchange(part, AWAY_Z),), cost=2**20)
-    owned = exchange(strips, PLANES).reshape(B, B)
+    owned = lax.all_to_all(strips, ("y", "x"), 0, 0).reshape(B, B)
 
     scaled, strips = call(
         direction_kernel,
         ((NEAR, B // NEAR, B), (NZ, B // NEAR, B)),
-        (here,),
+        (info,),
         (left_precond[0, 0], owned, right_precond[0, 0]),
         scratch=[pltpu.VMEM((NEAR, B // NEAR, B), jnp.float32)],
         cost=2**21,
     )
     scaled_other = lax.ppermute(scaled, "core", SWAP)
     strips = lax.all_to_all(strips, "zl", 0, 0)
-    direction = place(owner_table, here, [(0, 0, 0), (1, 0, 1)], [scaled, scaled_other])
-    foreign = call(foreign_kernel, (NEAR, NZ - 1, B // NEAR, B), (here,), (strips,), cost=2**20)
+    direction = place(info, [(0, 0, 0), (1, 0, 1)], [scaled, scaled_other])
+    foreign = call(foreign_kernel, (NEAR, NZ - 1, B // NEAR, B), (info,), (strips,), cost=2**20)
     foreign = exchange(foreign, QUADS)
     foreign_other = lax.ppermute(foreign, "core", SWAP)
     late = [(0, 1, 0), (0, 2, 0), (1, 1, 1), (1, 2, 1)]
-    direction = place(owner_table, here, late, [foreign, foreign_other], direction).reshape(NZ * NC, B, B)
+    direction = place(info, late, [foreign, foreign_other], direction).reshape(NZ * NC, B, B)
 
     outer_rows = lax.dot_general(
         owned, owned, (((1,), (1,)), ((), ())), preferred_element_type=jnp.float32

time: 118 us -> 117 us (level)
  the two profiles are of different devices: /device:TPU:1 before, /device:TPU:193 now
where the time goes in v3:
time: 117 us; the launch traced here: 116 us
  blocking collectives  89.8 us (77%)
  Pallas kernels  11.2 us (10%)
  starting transfers between devices  9.74 us (8%)
  matrix products  2.9 us (2%)
    all_to_all x3, blocking collectives, exchange(): return lax.all_to_all(pieces, SLAB, 0, 0, axis_index_groups=groups)  53.9 us
    all_to_all x1, blocking collectives, step(): owned = lax.all_to_all(strips, ('y', 'x'), 0, 0).reshape(B, B)  23 us
    all_to_all x1, blocking collectives, step(): strips = lax.all_to_all(strips, 'zl', 0, 0)  12.9 us
    pallas_call x7, Pallas kernels, call(): pl.pallas_call(kernel, out_shape=tuple((pltpu.VMEM(o, jnp.bfloat16) for o...  7.74 us
    ppermute x1, starting transfers between devices, step(): foreign_other = lax.ppermute(foreign, 'core', SWAP)  5.1 us
    pallas_call x2, Pallas kernels, place(): pl.pallas_call(functools.partial(place_kernel, parts), out_shape=jax.Shap...  3.45 us
    ppermute x1, starting transfers between devices, step(): got = lax.ppermute(give, 'core', SWAP)  2.58 us
  transfers between devices with their start and end apart: 3, of which 1 were waited for; matrix products, arithmetic and copies ran while one was open for 2% of the time, Pallas kernels for 3%

profile of v3, /device:TPU:193, one launch (start us, length us, event | category | flops | bytes accessed | tf_op | source)
XLA Modules:
  0.0 116.2 jit_solution(513022625722562222)
XLA Ops:
  0.7 0.7 pad_add_fusion.info_ref
  1.4 1.9 %shard_map.86 = bf16[3,512,512]{2,1,0:T(8,128)(2,1)S(1)} custom-call(s32[9]{0:T(128)S(1)} %pad_add_fusion.info_ref, bf16[6,512,512]{2,1,0:T(8,128)(2,1)} %bitcast.35), custom_call_target="tpu_custom_call" | custom-call | bytes 2097152 | tf_op jit(solution)/shard_map/pallas_call | solution.py:46
  3.3 2.6 %collective-permute-start = (bf16[3,512,512]{2,1,0:T(8,128)(2,1)S(1)}, bf16[3,512,512]{2,1,0:T(8,128)(2,1)S(1)}, u32[]{:S(2)}, u32[]{:S(2)}) collective-permute-start(bf16[3,512,512]{2,1,0:T(8,128)(2,1)S(1)} %shard_map.86), channel_id=1, source_target_pairs={{0,4},{4,0},{1,5},{5,1},{2,6},{6,2},{3,7},{7,3},{8,12},{12,8},{9,1... | collective-permute-start | bytes 4718600 | tf_op jit(solution)/shard_map/ppermute | solution.py:189
  5.9 1.9 %shard_map.85.keep_ref = bf16[3,512,512]{2,1,0:T(8,128)(2,1)S(1)} custom-call(s32[9]{0:T(128)S(1)} %pad_add_fusion.info_ref, bf16[6,512,512]{2,1,0:T(8,128)(2,1)} %bitcast.36), custom_call_target="tpu_custom_call" | custom-call | bytes 2097152 | tf_op jit(solution)/shard_map/pallas_call | solution.py:46
  7.9 1.1 collective-permute-done.got_ref
  8.9 0.9 shard_map.87
  9.9 17.7 %all_to_all.25.terms_ref = bf16[4,24,16,512]{3,2,1,0:T(8,128)(2,1)S(1)} all-to-all(bf16[4,24,16,512]{3,2,1,0:T(8,128)(2,1)S(1)} %bitcast.32), channel_id=1, replica_groups={{0,24,96,120},{48,72,144,168},{192,216,288,312},{240,264,336,360},{384,..., dimensions={0} | all-to-all | bytes 3145728 | tf_op jit(solution)/shard_map/all_to_all | solution.py:168
  27.5 0.2 shard_map.88
  27.8 0.0 copy-start
  27.8 0.0 copy-start.1
  27.8 23.2 %all_to_all.26.terms_ref = bf16[24,16,512]{2,1,0:T(8,128)(2,1)S(1)} all-to-all(bf16[24,16,512]{2,1,0:T(8,128)(2,1)S(1)} %shard_map.88), channel_id=1, replica_groups={{0,8,16,48,56,64,192,200,208,240,248,256,384,392,400,432,440,448,576,58..., dimensions={0} | all-to-all | bytes 786432 | tf_op jit(solution)/shard_map/all_to_all | solution.py:168
  51.0 0.1 shard_map.89
  51.1 23.0 %all_to_all.27 = bf16[32,16,512]{2,1,0:T(8,128)(2,1)S(1)} all-to-all(bf16[32,16,512]{2,1,0:T(8,128)(2,1)S(1)} %shard_map.89), channel_id=1, replica_groups=mesh['y'=8,'x'=4,'zl'=3,'core'=2,'tensor'=4] {'y','x'}, dimensions={0} | all-to-all | bytes 1048576 | tf_op jit(solution)/shard_map/all_to_all | solution.py:195
  74.2 2.0 %shard_map.90 = (bf16[4,128,512]{2,1,0:T(8,128)(2,1)S(1)}, bf16[3,128,512]{2,1,0:T(8,128)(2,1)S(1)}) custom-call(s32[9]{0:T(128)S(1)} %pad_add_fusion.info_ref, bf16[512,512]{1,0:T(8,128)(2,1)S(1)} %bitcast.33, bf16[512,512]{1,0:T(8,128)(2,1)S(1)} %bitcast.30, bf16[512,512]{1,0:T(8,128)(2,1)S(1)} %bitcast.34), custom_call_target="tpu_custom_call" | custom-call | bytes 2097152 | tf_op jit(solution)/shard_map/pallas_call | solution.py:46
  76.2 12.9 %all_to_all.28.strips_ref = bf16[3,128,512]{2,1,0:T(8,128)(2,1)S(1)} all-to-all(bf16[3,128,512]{2,1,0:T(8,128)(2,1)S(1)} %get-tuple-element.5), channel_id=1, replica_groups=mesh['y'=8,'x'=4,'zl'=3,'core'=2,'tensor'=4] {'zl'}, dimensions={0} | all-to-all | bytes 786432 | tf_op jit(solution)/shard_map/all_to_all | solution.py:206
  89.0 0.6 shard_map.91
  89.7 13.0 %all_to_all.29.refs_0_ = bf16[4,2,128,512]{3,2,1,0:T(8,128)(2,1)S(1)} all-to-all(bf16[4,2,128,512]{3,2,1,0:T(8,128)(2,1)S(1)} %shard_map.91), channel_id=1, replica_groups={{0,24,96,120},{48,72,144,168},{192,216,288,312},{240,264,336,360},{384,..., dimensions={0} | all-to-all | bytes 2097152 | tf_op jit(solution)/shard_map/all_to_all | solution.py:168
  102.7 5.1 %collective-permute-start.1 = (bf16[4,2,128,512]{3,2,1,0:T(8,128)(2,1)S(1)}, bf16[4,2,128,512]{3,2,1,0:T(8,128)(2,1)S(1)}, u32[]{:S(2)}, u32[]{:S(2)}) collective-permute-start(bf16[4,2,128,512]{3,2,1,0:T(8,128)(2,1)S(1)} %all_to_all.29.refs_0_), channel_id=1, source_target_pairs={{0,4},{4,0},{1,5},{5,1},{2,6},{6,2},{3,7},{7,3},{8,12},{12,8},{9,1... | collective-permute-start | bytes 3145736 | tf_op jit(solution)/shard_map/ppermute | solution.py:210
  107.8 0.0 copy-start.3
  107.8 2.1 %collective-permute-start.2 = (bf16[4,128,512]{2,1,0:T(8,128)(2,1)S(1)}, bf16[4,128,512]{2,1,0:T(8,128)(2,1)S(1)}, u32[]{:S(2)}, u32[]{:S(2)}) collective-permute-start(bf16[4,128,512]{2,1,0:T(8,128)(2,1)S(1)} %get-tuple-element.6.refs_0_), channel_id=1, source_target_pairs={{0,4},{4,0},{1,5},{5,1},{2,6},{6,2},{3,7},{7,3},{8,12},{12,8},{9,1... | collective-permute-start | bytes 1572872 | tf_op jit(solution)/shard_map/ppermute | solution.py:205
  109.9 1.4 %fusion.2 = f32[1,1,512,512]{3,2,1,0:T(8,128)} fusion(bf16[512,512]{1,0:T(8,128)(2,1)S(1)} %bitcast.31, f32[1,1,512,512]{3,2,1,0:T(8,128)S(1)} %copy-done.2), kind=kOutput, calls=%fused_computation.4 | convolution fusion | flops 269221888 | bytes 2621440 | tf_op jit(solution)/shard_map/dot_general | solution.py:214
  111.3 1.5 %fusion.4 = f32[1,1,512,512]{3,2,1,0:T(8,128)} fusion(bf16[32,16,512]{2,1,0:T(8,128)(2,1)S(1)} %all_to_all.27, f32[1,1,512,512]{3,2,1,0:T(8,128)S(1)} %copy-done.3), kind=kOutput, calls=%fused_computation.6 | convolution fusion | flops 269221888 | bytes 2621440 | tf_op jit(solution)/shard_map/dot_general | solution.py:218
  112.8 1.5 %place.2.refs_2_ = bf16[6,4,128,512]{3,2,1,0:T(8,128)(2,1)} custom-call(s32[9]{0:T(128)S(1)} %pad_add_fusion.info_ref, bf16[4,128,512]{2,1,0:T(8,128)(2,1)S(1)} %get-tuple-element.6.refs_0_, bf16[4,128,512]{2,1,0:T(8,128)(2,1)S(1)} %collective-permute-done.2.refs_1_), custom_call_target="tpu_custom_call" | custom-call | bytes 1048576 | tf_op jit(solution)/shard_map/place/pallas_call | solution.py:152
  114.3 1.9 %place.3 = bf16[6,4,128,512]{3,2,1,0:T(8,128)(2,1)} custom-call(s32[9]{0:T(128)S(1)} %pad_add_fusion.info_ref, bf16[4,2,128,512]{3,2,1,0:T(8,128)(2,1)S(1)} %all_to_all.29.refs_0_, bf16[4,2,128,512]{3,2,1,0:T(8,128)(2,1)S(1)} %collective-permute-done.1.refs_1_, bf16[6,4,128,512]{3,2,1,0:T(8,128)(2,1)} %place.2.refs_2_), custom_call_target="tpu_custom_call", output_to_operand_aliasing={{}: (3, {})} | custom-call | bytes 2097152 | tf_op jit(solution)/shard_map/place/pallas_call | solution.py:152
  (7 shorter events, 0.0 us)
Async XLA Ops:
  3.3 5.6 %collective-permute-start = (bf16[3,512,512]{2,1,0:T(8,128)(2,1)S(1)}, bf16[3,512,512]{2,1,0:T(8,128)(2,1)S(1)}, u32[]{:S(2)}, u32[]{:S(2)}) collective-permute-start(bf16[3,512,512]{2,1,0:T(8,128)(2,1)S(1)} %shard_map.86), channel_id=1, source_target_pairs={{0,4},{4,0},{1,5},{5,1},{2,6},{6,2},{3,7},{7,3},{8,12},{12,8},{9,1... | collective-permute-start | bytes 4718600 | tf_op jit(solution)/shard_map/ppermute | solution.py:189
  27.8 46.4 %copy-start = (bf16[1,1,512,512]{3,2,1,0:T(8,128)(2,1)S(1)}, bf16[1,1,512,512]{3,2,1,0:T(8,128)(2,1)}, u32[]{:S(2)}) copy-start(bf16[1,1,512,512]{3,2,1,0:T(8,128)(2,1)} %param.10) | copy-start | bytes 1572868
  27.8 46.3 %copy-start.1 = (bf16[1,1,512,512]{3,2,1,0:T(8,128)(2,1)S(1)}, bf16[1,1,512,512]{3,2,1,0:T(8,128)(2,1)}, u32[]{:S(2)}) copy-start(bf16[1,1,512,512]{3,2,1,0:T(8,128)(2,1)} %param.11) | copy-start | bytes 1572868
  89.0 20.8 %copy-start.2 = (f32[1,1,512,512]{3,2,1,0:T(8,128)S(1)}, f32[1,1,512,512]{3,2,1,0:T(8,128)}, u32[]{:S(2)}) copy-start(f32[1,1,512,512]{3,2,1,0:T(8,128)} %param.8) | copy-start | bytes 3145732
  102.7 11.6 %collective-permute-start.1 = (bf16[4,2,128,512]{3,2,1,0:T(8,128)(2,1)S(1)}, bf16[4,2,128,512]{3,2,1,0:T(8,128)(2,1)S(1)}, u32[]{:S(2)}, u32[]{:S(2)}) collective-permute-start(bf16[4,2,128,512]{3,2,1,0:T(8,128)(2,1)S(1)} %all_to_all.29.refs_0_), channel_id=1, source_target_pairs={{0,4},{4,0},{1,5},{5,1},{2,6},{6,2},{3,7},{7,3},{8,12},{12,8},{9,1... | collective-permute-start | bytes 3145736 | tf_op jit(solution)/shard_map/ppermute | solution.py:210
  107.8 3.5 %copy-start.3 = (f32[1,1,512,512]{3,2,1,0:T(8,128)S(1)}, f32[1,1,512,512]{3,2,1,0:T(8,128)}, u32[]{:S(2)}) copy-start(f32[1,1,512,512]{3,2,1,0:T(8,128)} %param.9) | copy-start | bytes 3145732
  107.8 5.0 %collective-permute-start.2 = (bf16[4,128,512]{2,1,0:T(8,128)(2,1)S(1)}, bf16[4,128,512]{2,1,0:T(8,128)(2,1)S(1)}, u32[]{:S(2)}, u32[]{:S(2)}) collective-permute-start(bf16[4,128,512]{2,1,0:T(8,128)(2,1)S(1)} %get-tuple-element.6.refs_0_), channel_id=1, source_target_pairs={{0,4},{4,0},{1,5},{5,1},{2,6},{6,2},{3,7},{7,3},{8,12},{12,8},{9,1... | collective-permute-start | bytes 1572872 | tf_op jit(solution)/shard_map/ppermute | solution.py:205

commit v4 on v3

--- a/solution.py
+++ b/solution.py
@@ -113,7 +113,7 @@
             out_ref[i, d - 1] = strip
 
 
-def direction_kernel(info_ref, left_ref, owned_ref, right_ref, out_ref, strips_ref, full_ref):
+def direction_kernel(info_ref, left_ref, owned_ref, right_ref, out_ref, strips_ref, full_ref, strip_ref, sem):
     step = B // NEAR
     square = jnp.zeros((8, 128), jnp.float32)
     for i in range(NEAR):
@@ -123,11 +123,14 @@
         full_ref[i] = full
         square = square + jnp.sum((full * full).reshape(step // 8, 8, B // 128, 128), axis=(0, 2))
     scale = lax.rsqrt(jnp.sum(square) * (1.0 / (B * B)) + epsilon)
+    strip_ref[...] = (full_ref[info_ref[2]] * scale).astype(strip_ref.dtype)
+    copies = [pltpu.make_async_copy(strip_ref, strips_ref.at[z], sem.at[z]) for z in range(NZ)]
+    for copy in copies:
+        copy.start()
     for i in range(NEAR):
         out_ref[i] = (full_ref[i] * scale).astype(out_ref.dtype)
-    strip = out_ref[info_ref[2]]
-    for z in range(NZ):
-        strips_ref[z] = strip
+    for copy in copies:
+        copy.wait()
 
 
 def place_kernel(parts, info_ref, *refs):
@@ -194,22 +197,35 @@
     strips = call(spread_kernel, (NEAR * AWAY, ROWS, B), (), (exchange(part, AWAY_Z),), cost=2**20)
     owned = lax.all_to_all(strips, ("y", "x"), 0, 0).reshape(B, B)
 
-    scaled, strips = call(
+    held = [
+        pltpu.with_memory_space_constraint(a, VMEM) for a in (left_precond[0, 0], owned, right_precond[0, 0])
+    ]
+    strip = (B // NEAR, B)
+    scaled, strips = pl.pallas_call(
         direction_kernel,
-        ((NEAR, B // NEAR, B), (NZ, B // NEAR, B)),
-        (info,),
-        (left_precond[0, 0], owned, right_precond[0, 0]),
-        scratch=[pltpu.VMEM((NEAR, B // NEAR, B), jnp.float32)],
-        cost=2**21,
-    )
+        out_shape=(
+            pltpu.VMEM((NEAR,) + strip, jnp.bfloat16),
+            jax.ShapeDtypeStruct((NZ,) + strip, jnp.bfloat16),
+        ),
+        in_specs=[pl.BlockSpec(memory_space=SMEM)] + [pl.BlockSpec(memory_space=VMEM)] * 3,
+        out_specs=(pl.BlockSpec(memory_space=VMEM), pl.BlockSpec(memory_space=pl.ANY)),
+        scratch_shapes=[
+            pltpu.VMEM((NEAR,) + strip, jnp.float32),
+            pltpu.VMEM(strip, jnp.bfloat16),
+            pltpu.SemaphoreType.DMA((NZ,)),
+        ],
+        compiler_params=pltpu.CompilerParams(vmem_limit_bytes=2**22),
+        cost_estimate=pl.CostEstimate(flops=4 * B**3, bytes_accessed=2**21, transcendentals=0),
+        name="scaled",
+    )(info, *held)
     scaled_other = lax.ppermute(scaled, "core", SWAP)
     strips = lax.all_to_all(strips, "zl", 0, 0)
     direction = place(info, [(0, 0, 0), (1, 0, 1)], [scaled, scaled_other])
     foreign = call(foreign_kernel, (NEAR, NZ - 1, B // NEAR, B), (info,), (strips,), cost=2**20)
     foreign = exchange(foreign, QUADS)
     foreign_other = lax.ppermute(foreign, "core", SWAP)
-    late = [(0, 1, 0), (0, 2, 0), (1, 1, 1), (1, 2, 1)]
-    direction = place(info, late, [foreign, foreign_other], direction).reshape(NZ * NC, B, B)
+    direction = place(info, [(0, 1, 0), (0, 2, 0)], [foreign], direction)
+    direction = place(info, [(0, 1, 1), (0, 2, 1)], [foreign_other], direction).reshape(NZ * NC, B, B)
 
     outer_rows = lax.dot_general(
         owned, owned, (((1,), (1,)), ((), ())), preferred_element_type=jnp.float32

time: 117 us -> 118 us (level)
  Pallas kernels: 11.2 us -> 12.9 us
    pallas_call x0 -> x1, Pallas kernels: none -> 2.53 us  [step(): pl.pallas_call(direction_kernel, out_shape=(pltpu.VMEM((NEAR,) + strip, j...]
    pallas_call x7 -> x6, Pallas kernels: 7.74 us -> 5.72 us  [call(): pl.pallas_call(kernel, out_shape=tuple((pltpu.VMEM(o, jnp.bfloat16) for o...]
    pallas_call x2 -> x3, Pallas kernels: 3.45 us -> 4.63 us  [place(): pl.pallas_call(functools.partial(place_kernel, parts), out_shape=jax.Shap...]
  transfers between devices with their start and end apart: 3 -> 3, of which waited for: 1 -> 1; matrix products, arithmetic and copies ran while one was open for 2% -> 2% of each run, Pallas kernels for 3% -> 4%
where the time goes in v4:
time: 118 us
  blocking collectives  89.8 us (76%)
  Pallas kernels  12.9 us (11%)
  starting transfers between devices  9.74 us (8%)
  matrix products  2.9 us (2%)
    all_to_all x3, blocking collectives, exchange(): return lax.all_to_all(pieces, SLAB, 0, 0, axis_index_groups=groups)  53.9 us
    all_to_all x1, blocking collectives, step(): owned = lax.all_to_all(strips, ('y', 'x'), 0, 0).reshape(B, B)  23 us
    all_to_all x1, blocking collectives, step(): strips = lax.all_to_all(strips, 'zl', 0, 0)  12.9 us
    pallas_call x6, Pallas kernels, call(): pl.pallas_call(kernel, out_shape=tuple((pltpu.VMEM(o, jnp.bfloat16) for o...  5.72 us
    ppermute x1, starting transfers between devices, step(): foreign_other = lax.ppermute(foreign, 'core', SWAP)  5.1 us
    pallas_call x3, Pallas kernels, place(): pl.pallas_call(functools.partial(place_kernel, parts), out_shape=jax.Shap...  4.63 us
    ppermute x1, starting transfers between devices, step(): got = lax.ppermute(give, 'core', SWAP)  2.58 us
    pallas_call x1, Pallas kernels, step(): pl.pallas_call(direction_kernel, out_shape=(pltpu.VMEM((NEAR,) + strip, j...  2.53 us
  transfers between devices with their start and end apart: 3, of which 1 were waited for; matrix products, arithmetic and copies ran while one was open for 2% of the time, Pallas kernels for 4%

profile of v4, /device:TPU:193, one launch (start us, length us, event | category | flops | bytes accessed | tf_op | source)
XLA Modules:
  0.0 117.9 jit_solution(13017291435308054555)
XLA Ops:
  0.7 0.7 pad_add_fusion.info_ref
  1.4 1.9 %shard_map.86 = bf16[3,512,512]{2,1,0:T(8,128)(2,1)S(1)} custom-call(s32[9]{0:T(128)S(1)} %pad_add_fusion.info_ref, bf16[6,512,512]{2,1,0:T(8,128)(2,1)} %bitcast.36), custom_call_target="tpu_custom_call" | custom-call | bytes 2097152 | tf_op jit(solution)/shard_map/pallas_call | solution.py:46
  3.3 2.6 %collective-permute-start = (bf16[3,512,512]{2,1,0:T(8,128)(2,1)S(1)}, bf16[3,512,512]{2,1,0:T(8,128)(2,1)S(1)}, u32[]{:S(2)}, u32[]{:S(2)}) collective-permute-start(bf16[3,512,512]{2,1,0:T(8,128)(2,1)S(1)} %shard_map.86), channel_id=1, source_target_pairs={{0,4},{4,0},{1,5},{5,1},{2,6},{6,2},{3,7},{7,3},{8,12},{12,8},{9,1... | collective-permute-start | bytes 4718600 | tf_op jit(solution)/shard_map/ppermute | solution.py:192
  5.9 1.9 %shard_map.85.keep_ref = bf16[3,512,512]{2,1,0:T(8,128)(2,1)S(1)} custom-call(s32[9]{0:T(128)S(1)} %pad_add_fusion.info_ref, bf16[6,512,512]{2,1,0:T(8,128)(2,1)} %bitcast.37), custom_call_target="tpu_custom_call" | custom-call | bytes 2097152 | tf_op jit(solution)/shard_map/pallas_call | solution.py:46
  7.9 1.1 collective-permute-done.got_ref
  8.9 0.9 shard_map.87
  9.9 17.7 %all_to_all.25.terms_ref = bf16[4,24,16,512]{3,2,1,0:T(8,128)(2,1)S(1)} all-to-all(bf16[4,24,16,512]{3,2,1,0:T(8,128)(2,1)S(1)} %bitcast.30), channel_id=1, replica_groups={{0,24,96,120},{48,72,144,168},{192,216,288,312},{240,264,336,360},{384,..., dimensions={0} | all-to-all | bytes 3145728 | tf_op jit(solution)/shard_map/all_to_all | solution.py:171
  27.5 0.2 shard_map.88
  27.8 0.0 copy-start
  27.8 23.2 %all_to_all.26.terms_ref = bf16[24,16,512]{2,1,0:T(8,128)(2,1)S(1)} all-to-all(bf16[24,16,512]{2,1,0:T(8,128)(2,1)S(1)} %shard_map.88), channel_id=1, replica_groups={{0,8,16,48,56,64,192,200,208,240,248,256,384,392,400,432,440,448,576,58..., dimensions={0} | all-to-all | bytes 786432 | tf_op jit(solution)/shard_map/all_to_all | solution.py:171
  51.0 0.1 shard_map.89
  51.1 23.0 %all_to_all.27 = bf16[32,16,512]{2,1,0:T(8,128)(2,1)S(1)} all-to-all(bf16[32,16,512]{2,1,0:T(8,128)(2,1)S(1)} %shard_map.89), channel_id=1, replica_groups=mesh['y'=8,'x'=4,'zl'=3,'core'=2,'tensor'=4] {'y','x'}, dimensions={0} | all-to-all | bytes 1048576 | tf_op jit(solution)/shard_map/all_to_all | solution.py:198
  74.2 2.5 %scaled.1 = (bf16[4,128,512]{2,1,0:T(8,128)(2,1)S(1)}, bf16[3,128,512]{2,1,0:T(8,128)(2,1)S(1)}) custom-call(s32[9]{0:T(128)S(1)} %pad_add_fusion.info_ref, bf16[512,512]{1,0:T(8,128)(2,1)S(1)} %bitcast.33, bf16[512,512]{1,0:T(8,128)(2,1)S(1)} %bitcast.31, bf16[512,512]{1,0:T(8,128)(2,1)S(1)} %bitcast.34), custom_call_target="tpu_custom_call" | custom-call | flops 536870912 | bytes 2097152 | tf_op jit(solution)/shard_map/scaled/pallas_call | solution.py:204
  76.7 12.9 %all_to_all.28.strips_ref = bf16[3,128,512]{2,1,0:T(8,128)(2,1)S(1)} all-to-all(bf16[3,128,512]{2,1,0:T(8,128)(2,1)S(1)} %get-tuple-element.5), channel_id=1, replica_groups=mesh['y'=8,'x'=4,'zl'=3,'core'=2,'tensor'=4] {'zl'}, dimensions={0} | all-to-all | bytes 786432 | tf_op jit(solution)/shard_map/all_to_all | solution.py:222
  89.6 0.6 shard_map.90
  90.2 13.0 %all_to_all.29.refs_0_ = bf16[4,2,128,512]{3,2,1,0:T(8,128)(2,1)S(1)} all-to-all(bf16[4,2,128,512]{3,2,1,0:T(8,128)(2,1)S(1)} %shard_map.90), channel_id=1, replica_groups={{0,24,96,120},{48,72,144,168},{192,216,288,312},{240,264,336,360},{384,..., dimensions={0} | all-to-all | bytes 2097152 | tf_op jit(solution)/shard_map/all_to_all | solution.py:171
  103.2 5.1 %collective-permute-start.1 = (bf16[4,2,128,512]{3,2,1,0:T(8,128)(2,1)S(1)}, bf16[4,2,128,512]{3,2,1,0:T(8,128)(2,1)S(1)}, u32[]{:S(2)}, u32[]{:S(2)}) collective-permute-start(bf16[4,2,128,512]{3,2,1,0:T(8,128)(2,1)S(1)} %all_to_all.29.refs_0_), channel_id=1, source_target_pairs={{0,4},{4,0},{1,5},{5,1},{2,6},{6,2},{3,7},{7,3},{8,12},{12,8},{9,1... | collective-permute-start | bytes 3145736 | tf_op jit(solution)/shard_map/ppermute | solution.py:226
  108.3 0.0 copy-start.3
  108.3 2.1 %collective-permute-start.2 = (bf16[4,128,512]{2,1,0:T(8,128)(2,1)S(1)}, bf16[4,128,512]{2,1,0:T(8,128)(2,1)S(1)}, u32[]{:S(2)}, u32[]{:S(2)}) collective-permute-start(bf16[4,128,512]{2,1,0:T(8,128)(2,1)S(1)} %get-tuple-element.6.refs_0_), channel_id=1, source_target_pairs={{0,4},{4,0},{1,5},{5,1},{2,6},{6,2},{3,7},{7,3},{8,12},{12,8},{9,1... | collective-permute-start | bytes 1572872 | tf_op jit(solution)/shard_map/ppermute | solution.py:221
  110.4 1.4 %fusion.2 = f32[1,1,512,512]{3,2,1,0:T(8,128)} fusion(bf16[512,512]{1,0:T(8,128)(2,1)S(1)} %bitcast.32, f32[1,1,512,512]{3,2,1,0:T(8,128)S(1)} %copy-done.2), kind=kOutput, calls=%fused_computation.4 | convolution fusion | flops 269221888 | bytes 2621440 | tf_op jit(solution)/shard_map/dot_general | solution.py:230
  111.8 1.5 %fusion.4 = f32[1,1,512,512]{3,2,1,0:T(8,128)} fusion(bf16[32,16,512]{2,1,0:T(8,128)(2,1)S(1)} %all_to_all.27, f32[1,1,512,512]{3,2,1,0:T(8,128)S(1)} %copy-done.3), kind=kOutput, calls=%fused_computation.6 | convolution fusion | flops 269221888 | bytes 2621440 | tf_op jit(solution)/shard_map/dot_general | solution.py:234
  113.3 1.5 %place.3.refs_1_ = bf16[6,4,128,512]{3,2,1,0:T(8,128)(2,1)} custom-call(s32[9]{0:T(128)S(1)} %pad_add_fusion.info_ref, bf16[4,128,512]{2,1,0:T(8,128)(2,1)S(1)} %get-tuple-element.6.refs_0_, bf16[4,128,512]{2,1,0:T(8,128)(2,1)S(1)} %collective-permute-done.2.refs_1_), custom_call_target="tpu_custom_call" | custom-call | bytes 1048576 | tf_op jit(solution)/shard_map/place/pallas_call | solution.py:155
  114.8 1.5 %place.4.refs_1_ = bf16[6,4,128,512]{3,2,1,0:T(8,128)(2,1)} custom-call(s32[9]{0:T(128)S(1)} %pad_add_fusion.info_ref, bf16[4,2,128,512]{3,2,1,0:T(8,128)(2,1)S(1)} %all_to_all.29.refs_0_, bf16[6,4,128,512]{3,2,1,0:T(8,128)(2,1)} %place.3.refs_1_), custom_call_target="tpu_custom_call", output_to_operand_aliasing={{}: (2, {})} | custom-call | bytes 1048576 | tf_op jit(solution)/shard_map/place/pallas_call | solution.py:155
  116.4 1.5 %place.5 = bf16[6,4,128,512]{3,2,1,0:T(8,128)(2,1)} custom-call(s32[9]{0:T(128)S(1)} %pad_add_fusion.info_ref, bf16[4,2,128,512]{3,2,1,0:T(8,128)(2,1)S(1)} %collective-permute-done.1.refs_0_, bf16[6,4,128,512]{3,2,1,0:T(8,128)(2,1)} %place.4.refs_1_), custom_call_target="tpu_custom_call", output_to_operand_aliasing={{}: (2, {})} | custom-call | bytes 1048576 | tf_op jit(solution)/shard_map/place/pallas_call | solution.py:155
  (8 shorter events, 0.0 us)
Async XLA Ops:
  3.3 5.6 %collective-permute-start = (bf16[3,512,512]{2,1,0:T(8,128)(2,1)S(1)}, bf16[3,512,512]{2,1,0:T(8,128)(2,1)S(1)}, u32[]{:S(2)}, u32[]{:S(2)}) collective-permute-start(bf16[3,512,512]{2,1,0:T(8,128)(2,1)S(1)} %shard_map.86), channel_id=1, source_target_pairs={{0,4},{4,0},{1,5},{5,1},{2,6},{6,2},{3,7},{7,3},{8,12},{12,8},{9,1... | collective-permute-start | bytes 4718600 | tf_op jit(solution)/shard_map/ppermute | solution.py:192
  27.8 46.4 %copy-start = (bf16[1,1,512,512]{3,2,1,0:T(8,128)(2,1)S(1)}, bf16[1,1,512,512]{3,2,1,0:T(8,128)(2,1)}, u32[]{:S(2)}) copy-start(bf16[1,1,512,512]{3,2,1,0:T(8,128)(2,1)} %param.10) | copy-start | bytes 1572868
  27.8 46.3 %copy-start.1 = (bf16[1,1,512,512]{3,2,1,0:T(8,128)(2,1)S(1)}, bf16[1,1,512,512]{3,2,1,0:T(8,128)(2,1)}, u32[]{:S(2)}) copy-start(bf16[1,1,512,512]{3,2,1,0:T(8,128)(2,1)} %param.11) | copy-start | bytes 1572868
  89.5 20.8 %copy-start.2 = (f32[1,1,512,512]{3,2,1,0:T(8,128)S(1)}, f32[1,1,512,512]{3,2,1,0:T(8,128)}, u32[]{:S(2)}) copy-start(f32[1,1,512,512]{3,2,1,0:T(8,128)} %param.8) | copy-start | bytes 3145732
  103.2 13.2 %collective-permute-start.1 = (bf16[4,2,128,512]{3,2,1,0:T(8,128)(2,1)S(1)}, bf16[4,2,128,512]{3,2,1,0:T(8,128)(2,1)S(1)}, u32[]{:S(2)}, u32[]{:S(2)}) collective-permute-start(bf16[4,2,128,512]{3,2,1,0:T(8,128)(2,1)S(1)} %all_to_all.29.refs_0_), channel_id=1, source_target_pairs={{0,4},{4,0},{1,5},{5,1},{2,6},{6,2},{3,7},{7,3},{8,12},{12,8},{9,1... | collective-permute-start | bytes 3145736 | tf_op jit(solution)/shard_map/ppermute | solution.py:226
  108.3 3.5 %copy-start.3 = (f32[1,1,512,512]{3,2,1,0:T(8,128)S(1)}, f32[1,1,512,512]{3,2,1,0:T(8,128)}, u32[]{:S(2)}) copy-start(f32[1,1,512,512]{3,2,1,0:T(8,128)} %param.9) | copy-start | bytes 3145732
  108.3 5.0 %collective-permute-start.2 = (bf16[4,128,512]{2,1,0:T(8,128)(2,1)S(1)}, bf16[4,128,512]{2,1,0:T(8,128)(2,1)S(1)}, u32[]{:S(2)}, u32[]{:S(2)}) collective-permute-start(bf16[4,128,512]{2,1,0:T(8,128)(2,1)S(1)} %get-tuple-element.6.refs_0_), channel_id=1, source_target_pairs={{0,4},{4,0},{1,5},{5,1},{2,6},{6,2},{3,7},{7,3},{8,12},{12,8},{9,1... | collective-permute-start | bytes 1572872 | tf_op jit(solution)/shard_map/ppermute | solution.py:221

commit v5 on v4

--- a/solution.py
+++ b/solution.py
@@ -30,7 +30,7 @@
 
 QUADS = [[device(c, z, f, q) for q in range(NEAR)] for c in range(NC) for z in range(NZ) for f in range(AWAY)]
 AWAY_Z = [
-    [device(c, z, f, q) for f in range(AWAY) for z in range(NZ)] for c in range(NC) for q in range(NEAR)
+    [device(c, z, f, q) for z in range(NZ) for f in range(AWAY)] for c in range(NC) for q in range(NEAR)
 ]
 
 
@@ -78,10 +78,10 @@
             up, right = lax.rem(y + NY - core, jnp.int32(NY)), lax.rem(x + NX - core, jnp.int32(NX))
             member = 2 * lax.rem(up, jnp.int32(2)) + lax.rem(right, jnp.int32(2))
             quad = 2 * (up >> 1) + (right >> 1)
-            rows = pl.ds((y * NX + x) * ROWS, ROWS)
+            rows = pl.ds((x * NY + y) * ROWS, ROWS)
             for z in range(NZ):
                 total = keep_ref[z, rows].astype(jnp.float32) + got_ref[z, rows].astype(jnp.float32)
-                out_ref[member, quad, z] = total.astype(out_ref.dtype)
+                out_ref[member, z, quad] = total.astype(out_ref.dtype)
 
 
 def sum_kernel(terms_ref, out_ref):
@@ -191,11 +191,11 @@
     give = fetch(True)
     got = lax.ppermute(give, "core", SWAP)
     keep = fetch(False)
-    pieces = call(pair_kernel, (NEAR, AWAY, NZ, ROWS, B), (info,), (keep, got), cost=2**22)
+    pieces = call(pair_kernel, (NEAR, NZ, AWAY, ROWS, B), (info,), (keep, got), cost=2**22)
     in_quad = exchange(pieces.reshape(NEAR, AWAY * NZ, ROWS, B), QUADS)
     part = call(sum_kernel, (AWAY * NZ, ROWS, B), (), (in_quad,), cost=2**21)
     strips = call(spread_kernel, (NEAR * AWAY, ROWS, B), (), (exchange(part, AWAY_Z),), cost=2**20)
-    owned = lax.all_to_all(strips, ("y", "x"), 0, 0).reshape(B, B)
+    owned = lax.all_to_all(strips, ("x", "y"), 0, 0).reshape(B, B)
 
     held = [
         pltpu.with_memory_space_constraint(a, VMEM) for a in (left_precond[0, 0], owned, right_precond[0, 0])

time: 118 us -> 119 us (level)
  starting transfers between devices: 9.74 us -> 11.8 us
  blocking collectives: 89.8 us -> 87.9 us
    all_to_all x1, blocking collectives: 23 us -> 19.8 us  [step(): owned = lax.all_to_all(strips, ('x', 'y'), 0, 0).reshape(B, B)]
    ppermute x1, starting transfers between devices: 5.1 us -> 7.19 us  [step(): foreign_other = lax.ppermute(foreign, 'core', SWAP)]
    all_to_all x3, blocking collectives: 53.9 us -> 55.5 us  [exchange(): return lax.all_to_all(pieces, SLAB, 0, 0, axis_index_groups=groups)]
where the time goes in v5:
time: 119 us; the launch traced here: 118 us
  blocking collectives  87.9 us (74%)
  Pallas kernels  12.9 us (11%)
  starting transfers between devices  11.8 us (10%)
  matrix products  2.91 us (2%)
    all_to_all x3, blocking collectives, exchange(): return lax.all_to_all(pieces, SLAB, 0, 0, axis_index_groups=groups)  55.5 us
    all_to_all x1, blocking collectives, step(): owned = lax.all_to_all(strips, ('x', 'y'), 0, 0).reshape(B, B)  19.8 us
    all_to_all x1, blocking collectives, step(): strips = lax.all_to_all(strips, 'zl', 0, 0)  12.6 us
    ppermute x1, starting transfers between devices, step(): foreign_other = lax.ppermute(foreign, 'core', SWAP)  7.19 us
    pallas_call x6, Pallas kernels, call(): pl.pallas_call(kernel, out_shape=tuple((pltpu.VMEM(o, jnp.bfloat16) for o...  5.71 us
    pallas_call x3, Pallas kernels, place(): pl.pallas_call(functools.partial(place_kernel, parts), out_shape=jax.Shap...  4.63 us
    ppermute x1, starting transfers between devices, step(): got = lax.ppermute(give, 'core', SWAP)  2.58 us
    pallas_call x1, Pallas kernels, step(): pl.pallas_call(direction_kernel, out_shape=(pltpu.VMEM((NEAR,) + strip, j...  2.53 us
  transfers between devices with their start and end apart: 3, of which 1 were waited for; matrix products, arithmetic and copies ran while one was open for 2% of the time, Pallas kernels for 4%

profile of v5, /device:TPU:193, one launch (start us, length us, event | category | flops | bytes accessed | tf_op | source)
XLA Modules:
  0.0 118.2 jit_solution(3023609748441040246)
XLA Ops:
  0.7 0.7 pad_add_fusion.info_ref
  1.4 1.9 %shard_map.86 = bf16[3,512,512]{2,1,0:T(8,128)(2,1)S(1)} custom-call(s32[9]{0:T(128)S(1)} %pad_add_fusion.info_ref, bf16[6,512,512]{2,1,0:T(8,128)(2,1)} %bitcast.36), custom_call_target="tpu_custom_call" | custom-call | bytes 2097152 | tf_op jit(solution)/shard_map/pallas_call | solution.py:46
  3.3 2.6 %collective-permute-start = (bf16[3,512,512]{2,1,0:T(8,128)(2,1)S(1)}, bf16[3,512,512]{2,1,0:T(8,128)(2,1)S(1)}, u32[]{:S(2)}, u32[]{:S(2)}) collective-permute-start(bf16[3,512,512]{2,1,0:T(8,128)(2,1)S(1)} %shard_map.86), channel_id=1, source_target_pairs={{0,4},{4,0},{1,5},{5,1},{2,6},{6,2},{3,7},{7,3},{8,12},{12,8},{9,1... | collective-permute-start | bytes 4718600 | tf_op jit(solution)/shard_map/ppermute | solution.py:192
  5.9 1.9 %shard_map.85.keep_ref = bf16[3,512,512]{2,1,0:T(8,128)(2,1)S(1)} custom-call(s32[9]{0:T(128)S(1)} %pad_add_fusion.info_ref, bf16[6,512,512]{2,1,0:T(8,128)(2,1)} %bitcast.37), custom_call_target="tpu_custom_call" | custom-call | bytes 2097152 | tf_op jit(solution)/shard_map/pallas_call | solution.py:46
  7.9 1.1 collective-permute-done.got_ref
  8.9 0.9 shard_map.87
  9.8 17.7 %all_to_all.25.terms_ref = bf16[4,24,16,512]{3,2,1,0:T(8,128)(2,1)S(1)} all-to-all(bf16[4,24,16,512]{3,2,1,0:T(8,128)(2,1)S(1)} %bitcast.30), channel_id=1, replica_groups={{0,24,96,120},{48,72,144,168},{192,216,288,312},{240,264,336,360},{384,..., dimensions={0} | all-to-all | bytes 3145728 | tf_op jit(solution)/shard_map/all_to_all | solution.py:171
  27.5 0.2 shard_map.88
  27.8 0.0 copy-start
  27.8 0.0 copy-start.1
  27.8 24.9 %all_to_all.26.terms_ref = bf16[24,16,512]{2,1,0:T(8,128)(2,1)S(1)} all-to-all(bf16[24,16,512]{2,1,0:T(8,128)(2,1)S(1)} %shard_map.88), channel_id=1, replica_groups={{0,48,192,240,384,432,576,624,8,56,200,248,392,440,584,632,16,64,208,25..., dimensions={0} | all-to-all | bytes 786432 | tf_op jit(solution)/shard_map/all_to_all | solution.py:171
  52.7 0.1 shard_map.89
  52.8 19.8 %all_to_all.27 = bf16[32,16,512]{2,1,0:T(8,128)(2,1)S(1)} all-to-all(bf16[32,16,512]{2,1,0:T(8,128)(2,1)S(1)} %shard_map.89), channel_id=1, replica_groups=mesh['y'=8,'x'=4,'zl'=3,'core'=2,'tensor'=4] {'x','y'}, dimensions={0} | all-to-all | bytes 1048576 | tf_op jit(solution)/shard_map/all_to_all | solution.py:198
  72.6 2.5 %scaled.1 = (bf16[4,128,512]{2,1,0:T(8,128)(2,1)S(1)}, bf16[3,128,512]{2,1,0:T(8,128)(2,1)S(1)}) custom-call(s32[9]{0:T(128)S(1)} %pad_add_fusion.info_ref, bf16[512,512]{1,0:T(8,128)(2,1)S(1)} %bitcast.33, bf16[512,512]{1,0:T(8,128)(2,1)S(1)} %bitcast.31, bf16[512,512]{1,0:T(8,128)(2,1)S(1)} %bitcast.34), custom_call_target="tpu_custom_call" | custom-call | flops 536870912 | bytes 2097152 | tf_op jit(solution)/shard_map/scaled/pallas_call | solution.py:204
  75.1 12.6 %all_to_all.28.strips_ref = bf16[3,128,512]{2,1,0:T(8,128)(2,1)S(1)} all-to-all(bf16[3,128,512]{2,1,0:T(8,128)(2,1)S(1)} %get-tuple-element.5), channel_id=1, replica_groups=mesh['y'=8,'x'=4,'zl'=3,'core'=2,'tensor'=4] {'zl'}, dimensions={0} | all-to-all | bytes 786432 | tf_op jit(solution)/shard_map/all_to_all | solution.py:222
  87.8 0.6 shard_map.90
  88.4 12.9 %all_to_all.29.refs_0_ = bf16[4,2,128,512]{3,2,1,0:T(8,128)(2,1)S(1)} all-to-all(bf16[4,2,128,512]{3,2,1,0:T(8,128)(2,1)S(1)} %shard_map.90), channel_id=1, replica_groups={{0,24,96,120},{48,72,144,168},{192,216,288,312},{240,264,336,360},{384,..., dimensions={0} | all-to-all | bytes 2097152 | tf_op jit(solution)/shard_map/all_to_all | solution.py:171
  101.3 7.2 %collective-permute-start.1 = (bf16[4,2,128,512]{3,2,1,0:T(8,128)(2,1)S(1)}, bf16[4,2,128,512]{3,2,1,0:T(8,128)(2,1)S(1)}, u32[]{:S(2)}, u32[]{:S(2)}) collective-permute-start(bf16[4,2,128,512]{3,2,1,0:T(8,128)(2,1)S(1)} %all_to_all.29.refs_0_), channel_id=1, source_target_pairs={{0,4},{4,0},{1,5},{5,1},{2,6},{6,2},{3,7},{7,3},{8,12},{12,8},{9,1... | collective-permute-start | bytes 3145736 | tf_op jit(solution)/shard_map/ppermute | solution.py:226
  108.5 2.1 %collective-permute-start.2 = (bf16[4,128,512]{2,1,0:T(8,128)(2,1)S(1)}, bf16[4,128,512]{2,1,0:T(8,128)(2,1)S(1)}, u32[]{:S(2)}, u32[]{:S(2)}) collective-permute-start(bf16[4,128,512]{2,1,0:T(8,128)(2,1)S(1)} %get-tuple-element.6.refs_0_), channel_id=1, source_target_pairs={{0,4},{4,0},{1,5},{5,1},{2,6},{6,2},{3,7},{7,3},{8,12},{12,8},{9,1... | collective-permute-start | bytes 1572872 | tf_op jit(solution)/shard_map/ppermute | solution.py:221
  110.6 1.4 %fusion.2 = f32[1,1,512,512]{3,2,1,0:T(8,128)} fusion(bf16[512,512]{1,0:T(8,128)(2,1)S(1)} %bitcast.32, f32[1,1,512,512]{3,2,1,0:T(8,128)S(1)} %copy-done.2), kind=kOutput, calls=%fused_computation.4 | convolution fusion | flops 269221888 | bytes 2621440 | tf_op jit(solution)/shard_map/dot_general | solution.py:230
  112.0 1.5 %fusion.4 = f32[1,1,512,512]{3,2,1,0:T(8,128)} fusion(bf16[32,16,512]{2,1,0:T(8,128)(2,1)S(1)} %all_to_all.27, f32[1,1,512,512]{3,2,1,0:T(8,128)S(1)} %copy-done.3), kind=kOutput, calls=%fused_computation.6 | convolution fusion | flops 269221888 | bytes 2621440 | tf_op jit(solution)/shard_map/dot_general | solution.py:234
  113.5 1.5 %place.3.refs_1_ = bf16[6,4,128,512]{3,2,1,0:T(8,128)(2,1)} custom-call(s32[9]{0:T(128)S(1)} %pad_add_fusion.info_ref, bf16[4,128,512]{2,1,0:T(8,128)(2,1)S(1)} %get-tuple-element.6.refs_0_, bf16[4,128,512]{2,1,0:T(8,128)(2,1)S(1)} %collective-permute-done.2.refs_1_), custom_call_target="tpu_custom_call" | custom-call | bytes 1048576 | tf_op jit(solution)/shard_map/place/pallas_call | solution.py:155
  115.0 1.5 %place.4.refs_1_ = bf16[6,4,128,512]{3,2,1,0:T(8,128)(2,1)} custom-call(s32[9]{0:T(128)S(1)} %pad_add_fusion.info_ref, bf16[4,2,128,512]{3,2,1,0:T(8,128)(2,1)S(1)} %all_to_all.29.refs_0_, bf16[6,4,128,512]{3,2,1,0:T(8,128)(2,1)} %place.3.refs_1_), custom_call_target="tpu_custom_call", output_to_operand_aliasing={{}: (2, {})} | custom-call | bytes 1048576 | tf_op jit(solution)/shard_map/place/pallas_call | solution.py:155
  116.6 1.5 %place.5 = bf16[6,4,128,512]{3,2,1,0:T(8,128)(2,1)} custom-call(s32[9]{0:T(128)S(1)} %pad_add_fusion.info_ref, bf16[4,2,128,512]{3,2,1,0:T(8,128)(2,1)S(1)} %collective-permute-done.1.refs_0_, bf16[6,4,128,512]{3,2,1,0:T(8,128)(2,1)} %place.4.refs_1_), custom_call_target="tpu_custom_call", output_to_operand_aliasing={{}: (2, {})} | custom-call | bytes 1048576 | tf_op jit(solution)/shard_map/place/pallas_call | solution.py:155
  (8 shorter events, 0.0 us)
Async XLA Ops:
  3.3 5.6 %collective-permute-start = (bf16[3,512,512]{2,1,0:T(8,128)(2,1)S(1)}, bf16[3,512,512]{2,1,0:T(8,128)(2,1)S(1)}, u32[]{:S(2)}, u32[]{:S(2)}) collective-permute-start(bf16[3,512,512]{2,1,0:T(8,128)(2,1)S(1)} %shard_map.86), channel_id=1, source_target_pairs={{0,4},{4,0},{1,5},{5,1},{2,6},{6,2},{3,7},{7,3},{8,12},{12,8},{9,1... | collective-permute-start | bytes 4718600 | tf_op jit(solution)/shard_map/ppermute | solution.py:192
  27.8 44.8 %copy-start = (bf16[1,1,512,512]{3,2,1,0:T(8,128)(2,1)S(1)}, bf16[1,1,512,512]{3,2,1,0:T(8,128)(2,1)}, u32[]{:S(2)}) copy-start(bf16[1,1,512,512]{3,2,1,0:T(8,128)(2,1)} %param.10) | copy-start | bytes 1572868
  27.8 44.8 %copy-start.1 = (bf16[1,1,512,512]{3,2,1,0:T(8,128)(2,1)S(1)}, bf16[1,1,512,512]{3,2,1,0:T(8,128)(2,1)}, u32[]{:S(2)}) copy-start(bf16[1,1,512,512]{3,2,1,0:T(8,128)(2,1)} %param.11) | copy-start | bytes 1572868
  87.8 22.8 %copy-start.2 = (f32[1,1,512,512]{3,2,1,0:T(8,128)S(1)}, f32[1,1,512,512]{3,2,1,0:T(8,128)}, u32[]{:S(2)}) copy-start(f32[1,1,512,512]{3,2,1,0:T(8,128)} %param.8) | copy-start | bytes 3145732
  101.3 15.3 %collective-permute-start.1 = (bf16[4,2,128,512]{3,2,1,0:T(8,128)(2,1)S(1)}, bf16[4,2,128,512]{3,2,1,0:T(8,128)(2,1)S(1)}, u32[]{:S(2)}, u32[]{:S(2)}) collective-permute-start(bf16[4,2,128,512]{3,2,1,0:T(8,128)(2,1)S(1)} %all_to_all.29.refs_0_), channel_id=1, source_target_pairs={{0,4},{4,0},{1,5},{5,1},{2,6},{6,2},{3,7},{7,3},{8,12},{12,8},{9,1... | collective-permute-start | bytes 3145736 | tf_op jit(solution)/shard_map/ppermute | solution.py:226
  108.5 3.5 %copy-start.3 = (f32[1,1,512,512]{3,2,1,0:T(8,128)S(1)}, f32[1,1,512,512]{3,2,1,0:T(8,128)}, u32[]{:S(2)}) copy-start(f32[1,1,512,512]{3,2,1,0:T(8,128)} %param.9) | copy-start | bytes 3145732
  108.5 5.0 %collective-permute-start.2 = (bf16[4,128,512]{2,1,0:T(8,128)(2,1)S(1)}, bf16[4,128,512]{2,1,0:T(8,128)(2,1)S(1)}, u32[]{:S(2)}, u32[]{:S(2)}) collective-permute-start(bf16[4,128,512]{2,1,0:T(8,128)(2,1)S(1)} %get-tuple-element.6.refs_0_), channel_id=1, source_target_pairs={{0,4},{4,0},{1,5},{5,1},{2,6},{6,2},{3,7},{7,3},{8,12},{12,8},{9,1... | collective-permute-start | bytes 1572872 | tf_op jit(solution)/shard_map/ppermute | solution.py:221
